TPU v7x, 256 devices: a whole 4x4x8 slice. The times are simulated.
256 devices in a mesh: row: 32 (over y, z_lo, core), col: 8 (over z_hi, x).
Axes of the slice: x: 4, y: 4, z: 8 (z_hi: 2, z_lo: 4; z = z_hi * 4 + z_lo), core: 2. Of those that a mesh axis runs over, the one named last changes fastest.
Arguments:
- integrals: bfloat16 [32768, 32768], P('row', 'col'), may hold values from -0.03125 to 0.03125
- amplitudes: bfloat16 [32768, 1024], P(('col', 'row')), may hold values from -6 to 6
- source: float32 [32768, 1024], P(('row', 'col')), may hold values from -6 to 6
- occ_energy: float32 [64], replicated, may hold values from -2.5 to -0.5
- vir_energy: float32 [512], replicated, may hold values from 0.3 to 3
- col_energy: float32 [1024], replicated, may hold values from 0.8 to 3
Outputs:
- new_amplitudes: float32 [32768, 1024], P(('row', 'col'))
All inputs are finite; a program needn't handle non-finite values.
Results may differ from a plain program's by a relative error of at most 0.0003.
Values may be sent and summed in bfloat16 or wider, within the bound.
No kernel may reach another device: no remote copies, remote signals or barrier semaphores. Data moves between devices by JAX's collectives and lax.ppermute only.
A program may use at most 128 MiB of HBM per device.

v0:
```python
import jax
import jax.numpy as jnp
from jax import lax
from jax.sharding import PartitionSpec as P

VIRT = 512


def summed_terms(integrals, gathered):
    local_rows = integrals.shape[0]
    occ_rows = local_rows // VIRT
    occ_cols = integrals.shape[1] // VIRT
    columns = gathered.shape[1]
    blocks = integrals.reshape(occ_rows, VIRT, occ_cols, VIRT)
    amp_blocks = gathered.reshape(occ_cols, VIRT, columns)
    exchange_part = lax.dot_general(
        blocks, amp_blocks, (((1, 2), (1, 0)), ((), ())), preferred_element_type=jnp.float32
    )
    exchange_part = exchange_part.reshape(local_rows, columns)

    def both_rows(start, count):
        cycle_part = jnp.dot(integrals, gathered, preferred_element_type=jnp.float32)
        return cycle_part + exchange_part

    return both_rows


def per_device(integrals, amplitudes, source, occ_energy, vir_energy, col_energy):
    gathered = lax.all_gather(amplitudes, "row", axis=0, tiled=True)
    out_rows = source.shape[0]
    both_rows = summed_terms(integrals, gathered)
    summed = lax.psum_scatter(
        both_rows(jnp.int32(0), lax.axis_size("col") * out_rows),
        "col",
        scatter_dimension=0,
        tiled=True,
    )
    first = (lax.axis_index("row") * lax.axis_size("col") + lax.axis_index("col")) * out_rows
    vir_all = jnp.tile(vir_energy, occ_energy.shape[0])
    occ_all = jnp.repeat(occ_energy, VIRT)
    vir_part = lax.dynamic_slice_in_dim(vir_all, first, out_rows, 0)
    occ_part = lax.dynamic_slice_in_dim(occ_all, first, out_rows, 0)
    denom = vir_part[:, None] - occ_part[:, None] + col_energy[None, :]
    return -(source + summed) / denom


def solution(mesh):
    in_specs = (P("row", "col"), P(("col", "row"), None), P(("row", "col"), None), P(), P(), P())
    out_specs = P(("row", "col"), None)
    return jax.shard_map(
        per_device, mesh=mesh, in_specs=in_specs, out_specs=out_specs, check_vma=False
    )
```

profile of v0, /device:TPU:8, one launch (start us, length us, event | category | flops | bytes accessed | tf_op | source)
XLA Modules:
  0.0 235.3 jit_solution(379378004681602848)
XLA Ops:
  6.5 0.0 copy-start
  6.5 0.0 all-gather.2.cloned.1.call-start
  6.5 0.7 all-gather.2.cloned.1.call-update
  7.3 0.0 reduce-scatter.2.cloned.1.call-start
  7.3 12.2 %copy.8 = bf16[128,8,8,512]{3,2,1,0:T(8,128)(2,1)} copy(bf16[128,8,8,512]{3,1,2,0:T(8,128)(2,1)} %bitcast.22) | data formatting | bytes 16777216
  19.5 7.2 %bitcast_bitcast_fusion = bf16[2,512,512,8]{1,3,2,0:T(8,128)(2,1)} fusion(bf16[2,512,8,512]{3,2,1,0:T(8,128)(2,1)} %bitcast.21), kind=kLoop, calls=%fused_computation | loop fusion | bytes 16777216 | tf_op jit(solution)/shard_map/dot_general | solution.py:16
  26.7 13.9 %copy.7 = bf16[2,512,512,8]{2,1,0,3:T(8,128)(2,1)} copy(bf16[2,512,512,8]{1,3,2,0:T(8,128)(2,1)} %bitcast_bitcast_fusion) | data formatting | bytes 16777216 | tf_op jit(solution)/shard_map/dot_general | solution.py:16
  40.6 40.0 %all-gather.2.cloned.1.call-done = bf16[4096,1024]{1,0:T(8,128)(2,1)} async-done(((bf16[128,1024]{1,0:T(8,128)(2,1)}), bf16[4096,1024]{1,0:T(8,128)(2,1)}) %all-gather.2.cloned.1.call-update) | async-done | bytes 8388624 | tf_op jit(solution)/shard_map/all_gather | solution.py:29
  80.5 0.0 copy-start.1
  80.5 0.0 copy-start.5
  80.5 12.7 %fusion = f32[1024,1024]{1,0:T(8,128)S(1)} fusion(bf16[1024,4096]{1,0:T(8,128)(2,1)} %param.6, bf16[4096,1024]{1,0:T(8,128)(2,1)} %all-gather.2.cloned.1.call-done), kind=kOutput, calls=%fused_computation.6 | convolution fusion | flops 8589934592 | bytes 20971520 | tf_op jit(solution)/shard_map/dot_general | solution.py:22
  93.3 0.0 copy-done.1
  93.3 0.0 copy-done.5
  93.3 0.0 copy-start.4
  93.3 0.0 copy-start.2
  93.3 0.0 copy-start.3
  93.4 10.4 %bitcast_add_fusion = f32[1024,1024]{1,0:T(8,128)} fusion(f32[1024,1024]{1,0:T(8,128)S(1)} %fusion, bf16[1024,512,8]{1,0,2:T(8,128)(2,1)S(1)} %bitcast.23, bf16[8,512,1024]{2,1,0:T(8,128)(2,1)S(1)} %bitcast.26), kind=kOutput, calls=%fused_computation.1 | convolution fusion | flops 8590983168 | bytes 25165824 | tf_op jit(solution)/shard_map/dot_general | solution.py:16
  103.7 0.0 reduce-scatter.2.cloned.1.call-update
  103.7 0.0 copy-done.4
  103.7 0.1 broadcast_bitcast_fusion
  103.9 0.0 copy-done
  103.9 0.1 dynamic-slice_subtract_fusion
  104.0 122.4 %reduce-scatter.2.cloned.1.call-done = f32[128,1024]{1,0:T(8,128)} async-done(((f32[1024,1024]{1,0:T(8,128)}), f32[128,1024]{1,0:T(8,128)}) %reduce-scatter.2.cloned.1.call-update) | async-done | bytes 524304 | tf_op jit(solution)/shard_map/reduce_scatter | solution.py:32
  226.4 0.0 copy-done.2
  226.4 0.0 copy-done.3
  226.4 2.0 add_divide_fusion
  (3 shorter events, 0.1 us)
Async XLA Ops:
  6.5 97.3 %copy-start = (f32[512]{0:T(512)S(1)}, f32[512]{0:T(512)}, u32[]{:S(2)}) copy-start(f32[512]{0:T(512)} %param.10) | copy-start | bytes 6148
  6.5 74.0 %all-gather.2.cloned.1.call-start = ((), (), s32[]{:S(2)}) async-start(), calls=%async_computation.1 | async-start | bytes 8650752 | tf_op jit(solution)/shard_map/all_gather | solution.py:29
  7.3 219.2 %reduce-scatter.2.cloned.1.call-start = ((), (), s32[]{:S(2)}) async-start(), calls=%async_computation.2 | async-start | bytes 4718592 | tf_op jit(solution)/shard_map/reduce_scatter | solution.py:32
  80.5 12.8 %copy-start.1 = (bf16[2,512,512,8]{2,1,0,3:T(8,128)(2,1)S(1)}, bf16[2,512,512,8]{2,1,0,3:T(8,128)(2,1)}, u32[]{:S(2)}) copy-start(bf16[2,512,512,8]{2,1,0,3:T(8,128)(2,1)} %copy.7) | copy-start | bytes 25165828
  80.5 12.8 %copy-start.5 = (bf16[4096,1024]{1,0:T(8,128)(2,1)S(1)}, bf16[4096,1024]{1,0:T(8,128)(2,1)}, u32[]{:S(2)}) copy-start(bf16[4096,1024]{1,0:T(8,128)(2,1)} %all-gather.2.cloned.1.call-done) | copy-start | bytes 25165828
  93.3 10.4 %copy-start.4 = (f32[64]{0:T(128)S(1)}, f32[64]{0:T(128)}, u32[]{:S(2)}) copy-start(f32[64]{0:T(128)} %param.9) | copy-start | bytes 772
  93.3 133.1 %copy-start.2 = (f32[128,1024]{1,0:T(8,128)S(1)}, f32[128,1024]{1,0:T(8,128)}, u32[]{:S(2)}) copy-start(f32[128,1024]{1,0:T(8,128)} %param.8) | copy-start | bytes 1572868
  93.3 133.1 %copy-start.3 = (f32[1024]{0:T(1024)S(1)}, f32[1024]{0:T(1024)}, u32[]{:S(2)}) copy-start(f32[1024]{0:T(1024)} %param.11) | copy-start | bytes 12292
Sparse Core Ops, SparseCore 0:
  9.2 71.3 all-gather.1
  103.9 122.5 reduce-scatter.1
where the time goes:
time: 236 us; the launch traced here: 235 us
  waiting for transfers between devices  163 us (69%)
  local copies, waits for them, and re-layouts  33.4 us (14%)
  matrix products  23.1 us (10%)
  between operations  13.5 us (6%)
    reduce_scatter x1, waiting for transfers between devices, per_device(): lax.psum_scatter(both_rows(jnp.int32(0), lax.axis_size('col') * out_rows)...  122 us
    all_gather x1, waiting for transfers between devices, per_device(): gathered = lax.all_gather(amplitudes, 'row', axis=0, tiled=True)  40 us
    dot_general x2, local copies, waits for them, and re-layouts, summed_terms(): lax.dot_general(blocks, amp_blocks, (((1, 2), (1, 0)), ((), ())), preferr...  21.1 us
    dot_general x1, matrix products, both_rows(): jnp.dot(integrals, gathered, preferred_element_type=jnp.float32)  12.7 us
    unnamed x17, local copies, waits for them, and re-layouts  12.4 us
    dot_general x1, matrix products, summed_terms(): lax.dot_general(blocks, amp_blocks, (((1, 2), (1, 0)), ((), ())), preferr...  10.4 us
  transfers between devices with their start and end apart: 2, of which 2 were waited for; matrix products, arithmetic and copies ran while one was open for 14% of the time, Pallas kernels for 0%

commit v1 on v0

v1 whole, which is shorter than its diff:
```python
import jax
import jax.numpy as jnp
import numpy as np
from jax import lax
from jax.experimental import pallas as pl
from jax.experimental.pallas import tpu as pltpu
from jax.sharding import PartitionSpec as P

VIRT = 512
ROWS, COLS = 32, 8
F8 = jnp.float8_e4m3fn
CHUNKS = (256, 256, 256, 256)
GATHER = ((2 << 1, 1 << 1), (1 << 1, 2 << 1), (1 << 3, 3 << 3), (3 << 3, 1 << 3))
REDUCE = ((1, 3), (3, 1))
SCALE = 8.0
LO = 2.0**17
A8 = 64.0


def row_perm(step):
    return [(r, r ^ step[r & 1]) for r in range(ROWS)]


def all_perm(step):
    pairs = []
    for r in range(ROWS):
        for c in range(COLS):
            pairs.append((r * COLS + c, r * COLS + (c ^ step[r & 1])))
    return pairs


def piece_table():
    table = np.zeros((ROWS, ROWS), np.int32)
    for r in range(ROWS):
        for p in range(ROWS):
            at = r ^ (p >> 4)
            for bit, step in enumerate(GATHER):
                if (p >> bit) & 1:
                    at ^= step[at & 1]
            table[r, p] = at
    return table


def tile_table():
    table = np.zeros((2, COLS, 8), np.int32)
    for core in range(2):
        for c in range(COLS):
            for q in range(8):
                q0, q1, q2 = q >> 2, (q >> 1) & 1, q & 1
                at = c ^ (q2 << 2)
                if q0:
                    at ^= REDUCE[0][core]
                if q1:
                    at ^= REDUCE[1][core]
                table[core, c, q] = at
    return table


def prep_kernel(x_ref, hi_ref, lo_ref):
    x = x_ref[...]
    both = (x.astype(jnp.float32) + x.T.astype(jnp.float32)) * SCALE
    hi = both.astype(jnp.bfloat16)
    hi_ref[...] = hi
    lo_ref[...] = ((both - hi.astype(jnp.float32)) * LO).astype(F8)


def prep(integrals):
    rows, depth = integrals.shape
    spec = pl.BlockSpec((VIRT, VIRT), lambda i, j: (i, j))
    return pl.pallas_call(
        prep_kernel,
        grid=(rows // VIRT, depth // VIRT),
        in_specs=[spec],
        out_specs=[spec, spec],
        out_shape=[
            jax.ShapeDtypeStruct((rows, depth), jnp.bfloat16),
            jax.ShapeDtypeStruct((rows, depth), F8),
        ],
        cost_estimate=pl.CostEstimate(flops=0, bytes_accessed=rows * depth * 5, transcendentals=0),
        name="prep",
    )(integrals)


def mm_kernel(table, hi_ref, lo_ref, mine, other, o_ref, a, a8, sems):
    block = mine.shape[0] // 16

    @pl.when(pl.program_id(0) == 0)
    def _():
        copies = []
        for p in range(32):
            src = mine if p < 16 else other
            at = pl.multiple_of(table[8 + p] * block, block)
            copies.append(
                pltpu.make_async_copy(
                    src.at[pl.ds((p % 16) * block, block)], a.at[pl.ds(at, block)], sems.at[p]
                )
            )
        for copy in copies:
            copy.start()
        for copy in copies:
            copy.wait()
        a8[...] = (a[...].astype(jnp.float32) * A8).astype(F8)

    main = jnp.dot(hi_ref[...], a[...], preferred_element_type=jnp.float32)
    rest = jnp.dot(lo_ref[...], a8[...], preferred_element_type=jnp.float32)
    o_ref[...] = main + rest * (1.0 / (LO * A8))


def mm(hi, lo, mine, other, table, half):
    depth, cols = hi.shape[1], mine.shape[1]
    tile = hi.shape[0] // 8
    m_spec = pl.BlockSpec((tile, depth), lambda i, t: (t[i + 4 * half], 0))
    hbm = pl.BlockSpec(memory_space=pl.ANY)
    return pl.pallas_call(
        mm_kernel,
        grid_spec=pltpu.PrefetchScalarGridSpec(
            num_scalar_prefetch=1,
            grid=(4,),
            in_specs=[m_spec, m_spec, hbm, hbm],
            out_specs=pl.BlockSpec((tile, cols), lambda i, t: (i, 0)),
            scratch_shapes=[
                pltpu.VMEM((depth, cols), jnp.bfloat16),
                pltpu.VMEM((depth, cols), F8),
                pltpu.SemaphoreType.DMA((32,)),
            ],
        ),
        out_shape=jax.ShapeDtypeStruct((4 * tile, cols), jnp.float32),
        cost_estimate=pl.CostEstimate(
            flops=12 * tile * depth * cols, bytes_accessed=tile * depth * 12, transcendentals=0
        ),
        name="mm",
    )(table, hi, lo, mine, other)


def gather(block):
    for step in GATHER:
        block = jnp.concatenate([block, lax.ppermute(block, "row", row_perm(step))], axis=0)
    return block, lax.ppermute(block, "row", row_perm((1, 1)))


def swap(value, step):
    sent = value.astype(jnp.float16)
    return lax.ppermute(sent, ("row", "col"), all_perm(step)).astype(jnp.float32)


def per_device(integrals, amplitudes, source, occ_energy, vir_energy, col_energy):
    row, col = lax.axis_index("row"), lax.axis_index("col")
    tiles = jnp.asarray(tile_table())[row & 1, col]
    pieces = jnp.asarray(piece_table())[row]
    table = jnp.concatenate([tiles, pieces])
    out_rows = source.shape[0]
    hi, lo = prep(integrals)
    sums = []
    start = 0
    for width in CHUNKS:
        mine, other = gather(amplitudes[:, start : start + width])
        send = mm(hi, lo, mine, other, table, 1)
        got = swap(send, REDUCE[0])
        keep = mm(hi, lo, mine, other, table, 0)
        half = 2 * out_rows
        got = swap(keep[half:] + got[half:], REDUCE[1]) + (keep[:half] + got[:half])
        sums.append(swap(got[out_rows:], (4, 4)) + got[:out_rows])
        start += width
    summed = jnp.concatenate(sums, axis=1) * (1.0 / SCALE)
    first = (row * COLS + col) * out_rows
    vir_all = jnp.tile(vir_energy, occ_energy.shape[0])
    occ_all = jnp.repeat(occ_energy, VIRT)
    vir_part = lax.dynamic_slice_in_dim(vir_all, first, out_rows, 0)
    occ_part = lax.dynamic_slice_in_dim(occ_all, first, out_rows, 0)
    denom = vir_part[:, None] - occ_part[:, None] + col_energy[None, :]
    return -(source + summed) / denom


def solution(mesh):
    in_specs = (P("row", "col"), P(("col", "row"), None), P(("row", "col"), None), P(), P(), P())
    out_specs = P(("row", "col"), None)
    return jax.shard_map(
        per_device, mesh=mesh, in_specs=in_specs, out_specs=out_specs, check_vma=False
    )
```

time: 236 us -> 186 us (0.79)
  waiting for transfers between devices: 163 us -> 18.8 us
  Pallas kernels: 0 us -> 81 us
  starting transfers between devices: 0.04 us -> 56.7 us
  local copies, waits for them, and re-layouts: 33.4 us -> 10.2 us
  matrix products: 23.1 us -> 0 us
  other arithmetic: 2.09 us -> 16.2 us
  between operations: 13.5 us -> 0.49 us
    reduce_scatter x1 -> x0, waiting for transfers between devices: 122 us -> none  [per_device(): lax.psum_scatter(both_rows(jnp.int32(0), lax.axis_size('col') * out_rows)...]
    pallas_call x0 -> x9, Pallas kernels: none -> 81 us  [the longest x8 65.6 us: mm(): pl.pallas_call(mm_kernel, grid_spec=pltpu.PrefetchScalarGridSpec(num_scal...]
    ppermute x0 -> x32, starting transfers between devices: none -> 56.7 us  [the longest x12 24.5 us: swap(): lax.ppermute(sent, ('row', 'col'), all_perm(step)).astype(jnp.float32)]
    all_gather x1 -> x0, waiting for transfers between devices: 40 us -> none  [per_device(): gathered = lax.all_gather(amplitudes, 'row', axis=0, tiled=True)]
    dot_general x2 -> x0, matrix products: 23.1 us -> none  [the longest x1 12.7 us: both_rows(): jnp.dot(integrals, gathered, preferred_element_type=jnp.float32)]
    dot_general x2 -> x0, local copies, waits for them, and re-layouts: 21.1 us -> none  [summed_terms(): lax.dot_general(blocks, amp_blocks, (((1, 2), (1, 0)), ((), ())), preferr...]
    ppermute x0 -> x32, waiting for transfers between devices: none -> 18.8 us  [the longest x16 10.6 us: gather(): lax.ppermute(block, 'row', row_perm(step))]
    convert_element_type x0 -> x12, other arithmetic: none -> 8.3 us  [the longest x8 6.17 us: swap(): sent = value.astype(jnp.float16)]
  transfers between devices with their start and end apart: 2 -> 32, of which waited for: 2 -> 9; matrix products, arithmetic and copies ran while one was open for 14% -> 13% of each run, Pallas kernels for 0% -> 44%
where the time goes in v1:
time: 186 us; the launch traced here: 183 us
  Pallas kernels  81 us (44%)
  starting transfers between devices  56.7 us (30%)
  waiting for transfers between devices  18.8 us (10%)
  other arithmetic  16.2 us (9%)
  local copies, waits for them, and re-layouts  10.2 us (5%)
    pallas_call x8, Pallas kernels, mm(): pl.pallas_call(mm_kernel, grid_spec=pltpu.PrefetchScalarGridSpec(num_scal...  65.6 us
    ppermute x12, starting transfers between devices, swap(): lax.ppermute(sent, ('row', 'col'), all_perm(step)).astype(jnp.float32)  24.5 us
    ppermute x16, starting transfers between devices, gather(): lax.ppermute(block, 'row', row_perm(step))  24.4 us
    pallas_call x1, Pallas kernels, prep(): pl.pallas_call(prep_kernel, grid=(rows // VIRT, depth // VIRT), in_specs=...  15.5 us
    ppermute x16, waiting for transfers between devices, gather(): lax.ppermute(block, 'row', row_perm(step))  10.6 us
    ppermute x12, waiting for transfers between devices, swap(): lax.ppermute(sent, ('row', 'col'), all_perm(step)).astype(jnp.float32)  8.17 us
    ppermute x4, starting transfers between devices, gather(): return (block, lax.ppermute(block, 'row', row_perm((1, 1))))  7.84 us
    unnamed x38, local copies, waits for them, and re-layouts  6.23 us
  transfers between devices with their start and end apart: 32, of which 9 were waited for; matrix products, arithmetic and copies ran while one was open for 13% of the time, Pallas kernels for 44%

profile of v1, /device:TPU:8, one launch (start us, length us, event | category | flops | bytes accessed | tf_op | source)
XLA Modules:
  0.0 183.4 jit_solution(3609099828316069781)
XLA Ops:
  0.0 1.6 fusion.11
  1.6 3.3 %collective-permute-start = (bf16[128,256]{1,0:T(8,128)(2,1)S(1)}, bf16[128,256]{1,0:T(8,128)(2,1)}, u32[]{:S(2)}, u32[]{:S(2)}) collective-permute-start(bf16[128,256]{1,0:T(8,128)(2,1)S(1)} %get-tuple-element.9), channel_id=1, source_target_pairs={{0,32},{8,24},{16,48},{24,8},{32,0},{40,56},{48,16},{56,40},{64,96... | collective-permute-start | bytes 196616 | tf_op jit(solution)/shard_map/ppermute | solution.py:137
  4.9 2.9 %collective-permute-start.16 = (bf16[128,256]{1,0:T(8,128)(2,1)S(1)}, bf16[128,256]{1,0:T(8,128)(2,1)S(1)}, u32[]{:S(2)}, u32[]{:S(2)}) collective-permute-start(bf16[128,256]{1,0:T(8,128)(2,1)S(1)} %get-tuple-element.16), channel_id=1, source_target_pairs={{0,32},{8,24},{16,48},{24,8},{32,0},{40,56},{48,16},{56,40},{64,96... | collective-permute-start | bytes 196616 | tf_op jit(solution)/shard_map/ppermute | solution.py:137
  8.5 15.5 %prep.1 = (bf16[1024,4096]{1,0:T(8,128)(2,1)}, f8e4m3fn[1024,4096]{1,0:T(32,128)(4,1)}) custom-call(bf16[1024,4096]{1,0:T(8,128)(2,1)} %x_ref.1), custom_call_target="tpu_custom_call" | custom-call | bytes 20971520 | tf_op jit(solution)/shard_map/prep/pallas_call | solution.py:70
  24.0 1.6 copy.9
  26.4 2.0 %collective-permute-start.1 = (bf16[256,256]{1,0:T(8,128)(2,1)S(1)}, bf16[256,256]{1,0:T(8,128)(2,1)S(1)}, u32[]{:S(2)}, u32[]{:S(2)}) collective-permute-start(bf16[256,256]{1,0:T(8,128)(2,1)S(1)} %pad_maximum_fusion.8), channel_id=1, source_target_pairs={{0,16},{8,40},{16,0},{24,56},{32,48},{40,8},{48,32},{56,24},{64,80... | collective-permute-start | bytes 393224 | tf_op jit(solution)/shard_map/ppermute | solution.py:137
  29.5 2.0 %collective-permute-start.17 = (bf16[256,256]{1,0:T(8,128)(2,1)S(1)}, bf16[256,256]{1,0:T(8,128)(2,1)S(1)}, u32[]{:S(2)}, u32[]{:S(2)}) collective-permute-start(bf16[256,256]{1,0:T(8,128)(2,1)S(1)} %pad_maximum_fusion.10), channel_id=1, source_target_pairs={{0,16},{8,40},{16,0},{24,56},{32,48},{40,8},{48,32},{56,24},{64,80... | collective-permute-start | bytes 393224 | tf_op jit(solution)/shard_map/ppermute | solution.py:137
  31.7 1.5 constant_dynamic-update-slice_fusion.3
  34.9 1.9 %collective-permute-start.2 = (bf16[512,256]{1,0:T(8,128)(2,1)S(1)}, bf16[512,256]{1,0:T(8,128)(2,1)S(1)}, u32[]{:S(2)}, u32[]{:S(2)}) collective-permute-start(bf16[512,256]{1,0:T(8,128)(2,1)S(1)} %pad_maximum_fusion.4), channel_id=1, source_target_pairs={{0,64},{8,200},{16,80},{24,216},{32,96},{40,232},{48,112},{56,248}... | collective-permute-start | bytes 786440 | tf_op jit(solution)/shard_map/ppermute | solution.py:137
  38.6 1.3 collective-permute-start.18
  40.0 1.0 collective-permute-start.26
  41.8 0.9 pad_maximum_fusion
  42.7 2.0 %collective-permute-start.3 = (bf16[1024,256]{1,0:T(8,128)(2,1)S(1)}, bf16[1024,256]{1,0:T(8,128)(2,1)S(1)}, u32[]{:S(2)}, u32[]{:S(2)}) collective-permute-start(bf16[1024,256]{1,0:T(8,128)(2,1)S(1)} %pad_maximum_fusion), channel_id=1, source_target_pairs={{0,192},{8,72},{16,208},{24,88},{32,224},{40,104},{48,240},{56,120... | collective-permute-start | bytes 1572872 | tf_op jit(solution)/shard_map/ppermute | solution.py:137
  44.7 0.9 pad_maximum_fusion.1
  45.6 1.9 %collective-permute-start.11 = (bf16[1024,256]{1,0:T(8,128)(2,1)S(1)}, bf16[1024,256]{1,0:T(8,128)(2,1)S(1)}, u32[]{:S(2)}, u32[]{:S(2)}) collective-permute-start(bf16[1024,256]{1,0:T(8,128)(2,1)S(1)} %pad_maximum_fusion.1), channel_id=1, source_target_pairs={{0,192},{8,72},{16,208},{24,88},{32,224},{40,104},{48,240},{56,120... | collective-permute-start | bytes 1572872 | tf_op jit(solution)/shard_map/ppermute | solution.py:137
  47.5 2.2 %collective-permute-done.18 = bf16[512,256]{1,0:T(8,128)(2,1)S(1)} collective-permute-done((bf16[512,256]{1,0:T(8,128)(2,1)S(1)}, bf16[512,256]{1,0:T(8,128)(2,1)S(1)}, u32[]{:S(2)}, u32[]{:S(2)}) %collective-permute-start.18) | collective-permute-done | bytes 262176 | tf_op jit(solution)/shard_map/ppermute | solution.py:137
  49.7 2.6 %collective-permute-start.19 = (bf16[1024,256]{1,0:T(8,128)(2,1)S(1)}, bf16[1024,256]{1,0:T(8,128)(2,1)S(1)}, u32[]{:S(2)}, u32[]{:S(2)}) collective-permute-start(bf16[1024,256]{1,0:T(8,128)(2,1)S(1)} %pad_maximum_fusion.2), channel_id=1, source_target_pairs={{0,192},{8,72},{16,208},{24,88},{32,224},{40,104},{48,240},{56,120... | collective-permute-start | bytes 1572872 | tf_op jit(solution)/shard_map/ppermute | solution.py:137
  52.3 3.0 %collective-permute-done.26 = bf16[512,256]{1,0:T(8,128)(2,1)S(1)} collective-permute-done((bf16[512,256]{1,0:T(8,128)(2,1)S(1)}, bf16[512,256]{1,0:T(8,128)(2,1)S(1)}, u32[]{:S(2)}, u32[]{:S(2)}) %collective-permute-start.26) | collective-permute-done | bytes 262176 | tf_op jit(solution)/shard_map/ppermute | solution.py:137
  55.3 2.6 %collective-permute-start.27 = (bf16[1024,256]{1,0:T(8,128)(2,1)S(1)}, bf16[1024,256]{1,0:T(8,128)(2,1)S(1)}, u32[]{:S(2)}, u32[]{:S(2)}) collective-permute-start(bf16[1024,256]{1,0:T(8,128)(2,1)S(1)} %pad_maximum_fusion.3), channel_id=1, source_target_pairs={{0,192},{8,72},{16,208},{24,88},{32,224},{40,104},{48,240},{56,120... | collective-permute-start | bytes 1572872 | tf_op jit(solution)/shard_map/ppermute | solution.py:137
  59.6 1.7 collective-permute-start.12
  61.3 2.5 %collective-permute-done.19 = bf16[1024,256]{1,0:T(8,128)(2,1)S(1)} collective-permute-done((bf16[1024,256]{1,0:T(8,128)(2,1)S(1)}, bf16[1024,256]{1,0:T(8,128)(2,1)S(1)}, u32[]{:S(2)}, u32[]{:S(2)}) %collective-permute-start.19) | collective-permute-done | bytes 524320 | tf_op jit(solution)/shard_map/ppermute | solution.py:137
  63.8 3.1 %collective-permute-start.20 = (bf16[2048,256]{1,0:T(8,128)(2,1)S(1)}, bf16[2048,256]{1,0:T(8,128)(2,1)}, u32[]{:S(2)}, u32[]{:S(2)}) collective-permute-start(bf16[2048,256]{1,0:T(8,128)(2,1)S(1)} %constant_dynamic-update-slice_fusion.10.mine), channel_id=1, source_target_pairs={{0,8},{8,0},{16,24},{24,16},{32,40},{40,32},{48,56},{56,48},{64,72... | collective-permute-start | bytes 3145736 | tf_op jit(solution)/shard_map/ppermute | solution.py:138
  66.9 2.5 %collective-permute-done.27 = bf16[1024,256]{1,0:T(8,128)(2,1)S(1)} collective-permute-done((bf16[1024,256]{1,0:T(8,128)(2,1)S(1)}, bf16[1024,256]{1,0:T(8,128)(2,1)S(1)}, u32[]{:S(2)}, u32[]{:S(2)}) %collective-permute-start.27) | collective-permute-done | bytes 524320 | tf_op jit(solution)/shard_map/ppermute | solution.py:137
  69.4 3.0 %collective-permute-start.28 = (bf16[2048,256]{1,0:T(8,128)(2,1)S(1)}, bf16[2048,256]{1,0:T(8,128)(2,1)}, u32[]{:S(2)}, u32[]{:S(2)}) collective-permute-start(bf16[2048,256]{1,0:T(8,128)(2,1)S(1)} %constant_dynamic-update-slice_fusion.15.mine), channel_id=1, source_target_pairs={{0,8},{8,0},{16,24},{24,16},{32,40},{40,32},{48,56},{56,48},{64,72... | collective-permute-start | bytes 3145736 | tf_op jit(solution)/shard_map/ppermute | solution.py:138
  75.3 8.2 %mm.9 = f32[512,256]{1,0:T(8,128)} custom-call(s32[40]{0:T(128)} %pad_add_fusion.table, bf16[1024,4096]{1,0:T(8,128)(2,1)} %get-tuple-element.7.hi_ref, f8e4m3fn[1024,4096]{1,0:T(32,128)(4,1)} %get-tuple-element.8.lo_ref, bf16[2048,256]{1,0:T(8,128)(2,1)} %constant_dynamic-update-slice_fusion.mine, bf16[2048,256]{1,0:T(8,128)(2,1)} %collective-permute-done.4.other), custom_call_target="tpu_custom_call" | custom-call | flops 1610612736 | bytes 6291456 | tf_op jit(solution)/shard_map/mm/pallas_call | solution.py:114
  83.5 1.8 convert_element_type.64
  85.3 1.5 collective-permute-start.5
  86.8 8.2 %mm.11 = f32[512,256]{1,0:T(8,128)} custom-call(s32[40]{0:T(128)} %pad_add_fusion.table, bf16[1024,4096]{1,0:T(8,128)(2,1)} %get-tuple-element.7.hi_ref, f8e4m3fn[1024,4096]{1,0:T(32,128)(4,1)} %get-tuple-element.8.lo_ref, bf16[2048,256]{1,0:T(8,128)(2,1)} %copy-done.3, bf16[2048,256]{1,0:T(8,128)(2,1)} %collective-permute-done.12.other), custom_call_target="tpu_custom_call" | custom-call | flops 1610612736 | bytes 6291456 | tf_op jit(solution)/shard_map/mm/pallas_call | solution.py:114
  95.0 1.1 convert_element_type.69
  96.7 8.2 %mm.13 = f32[512,256]{1,0:T(8,128)} custom-call(s32[40]{0:T(128)} %pad_add_fusion.table, bf16[1024,4096]{1,0:T(8,128)(2,1)} %get-tuple-element.7.hi_ref, f8e4m3fn[1024,4096]{1,0:T(32,128)(4,1)} %get-tuple-element.8.lo_ref, bf16[2048,256]{1,0:T(8,128)(2,1)} %copy-done.2, bf16[2048,256]{1,0:T(8,128)(2,1)} %collective-permute-done.20.other), custom_call_target="tpu_custom_call" | custom-call | flops 1610612736 | bytes 6291456 | tf_op jit(solution)/shard_map/mm/pallas_call | solution.py:114
  104.9 1.1 convert_element_type.74
  105.9 1.6 collective-permute-start.21
  107.5 8.2 %mm.15 = f32[512,256]{1,0:T(8,128)} custom-call(s32[40]{0:T(128)} %pad_add_fusion.table, bf16[1024,4096]{1,0:T(8,128)(2,1)} %get-tuple-element.7.hi_ref, f8e4m3fn[1024,4096]{1,0:T(32,128)(4,1)} %get-tuple-element.8.lo_ref, bf16[2048,256]{1,0:T(8,128)(2,1)} %copy-done.1, bf16[2048,256]{1,0:T(8,128)(2,1)} %collective-permute-done.28.other), custom_call_target="tpu_custom_call" | custom-call | flops 1610612736 | bytes 6291456 | tf_op jit(solution)/shard_map/mm/pallas_call | solution.py:114
  115.7 1.1 convert_element_type.79
  117.4 8.2 %mm.8 = f32[512,256]{1,0:T(8,128)} custom-call(s32[40]{0:T(128)} %pad_add_fusion.table, bf16[1024,4096]{1,0:T(8,128)(2,1)} %get-tuple-element.7.hi_ref, f8e4m3fn[1024,4096]{1,0:T(32,128)(4,1)} %get-tuple-element.8.lo_ref, bf16[2048,256]{1,0:T(8,128)(2,1)} %constant_dynamic-update-slice_fusion.mine, bf16[2048,256]{1,0:T(8,128)(2,1)} %collective-permute-done.4.other), custom_call_target="tpu_custom_call" | custom-call | flops 1610612736 | bytes 6291456 | tf_op jit(solution)/shard_map/mm/pallas_call | solution.py:114
  125.6 8.2 %mm.10 = f32[512,256]{1,0:T(8,128)} custom-call(s32[40]{0:T(128)} %pad_add_fusion.table, bf16[1024,4096]{1,0:T(8,128)(2,1)} %get-tuple-element.7.hi_ref, f8e4m3fn[1024,4096]{1,0:T(32,128)(4,1)} %get-tuple-element.8.lo_ref, bf16[2048,256]{1,0:T(8,128)(2,1)} %copy-done.3, bf16[2048,256]{1,0:T(8,128)(2,1)} %collective-permute-done.12.other), custom_call_target="tpu_custom_call" | custom-call | flops 1610612736 | bytes 6291456 | tf_op jit(solution)/shard_map/mm/pallas_call | solution.py:114
  133.8 8.2 %mm.12 = f32[512,256]{1,0:T(8,128)} custom-call(s32[40]{0:T(128)} %pad_add_fusion.table, bf16[1024,4096]{1,0:T(8,128)(2,1)} %get-tuple-element.7.hi_ref, f8e4m3fn[1024,4096]{1,0:T(32,128)(4,1)} %get-tuple-element.8.lo_ref, bf16[2048,256]{1,0:T(8,128)(2,1)} %copy-done.2, bf16[2048,256]{1,0:T(8,128)(2,1)} %collective-permute-done.20.other), custom_call_target="tpu_custom_call" | custom-call | flops 1610612736 | bytes 6291456 | tf_op jit(solution)/shard_map/mm/pallas_call | solution.py:114
  142.0 8.3 %mm.14 = f32[512,256]{1,0:T(8,128)} custom-call(s32[40]{0:T(128)} %pad_add_fusion.table, bf16[1024,4096]{1,0:T(8,128)(2,1)} %get-tuple-element.7.hi_ref, f8e4m3fn[1024,4096]{1,0:T(32,128)(4,1)} %get-tuple-element.8.lo_ref, bf16[2048,256]{1,0:T(8,128)(2,1)} %copy-done.1, bf16[2048,256]{1,0:T(8,128)(2,1)} %collective-permute-done.28.other), custom_call_target="tpu_custom_call" | custom-call | flops 1610612736 | bytes 6291456 | tf_op jit(solution)/shard_map/mm/pallas_call | solution.py:114
  150.4 1.1 convert_element_type.65
  151.5 3.1 %collective-permute-start.6 = (f16[256,256]{1,0:T(8,128)(2,1)S(1)}, f16[256,256]{1,0:T(8,128)(2,1)S(1)}, u32[]{:S(2)}, u32[]{:S(2)}) collective-permute-start(f16[256,256]{1,0:T(8,128)(2,1)S(1)} %fusion.10), channel_id=1, source_target_pairs={{0,3},{1,2},{2,1},{3,0},{4,7},{5,6},{6,5},{7,4},{8,9},{9,8},{10,11... | collective-permute-start | bytes 393224 | tf_op jit(solution)/shard_map/ppermute | solution.py:143
  155.2 1.0 convert_element_type.75
  156.3 2.8 %collective-permute-start.22 = (f16[256,256]{1,0:T(8,128)(2,1)S(1)}, f16[256,256]{1,0:T(8,128)(2,1)S(1)}, u32[]{:S(2)}, u32[]{:S(2)}) collective-permute-start(f16[256,256]{1,0:T(8,128)(2,1)S(1)} %fusion.6), channel_id=1, source_target_pairs={{0,3},{1,2},{2,1},{3,0},{4,7},{5,6},{6,5},{7,4},{8,9},{9,8},{10,11... | collective-permute-start | bytes 393224 | tf_op jit(solution)/shard_map/ppermute | solution.py:143
  159.2 1.0 fusion.4
  160.8 6.9 %collective-permute-start.7 = (f16[128,256]{1,0:T(8,128)(2,1)S(1)}, f16[128,256]{1,0:T(8,128)(2,1)S(1)}, u32[]{:S(2)}, u32[]{:S(2)}) collective-permute-start(f16[128,256]{1,0:T(8,128)(2,1)S(1)} %slice_convert_fusion.3), channel_id=1, source_target_pairs={{0,4},{1,5},{2,6},{3,7},{4,0},{5,1},{6,2},{7,3},{8,12},{9,13},{10,... | collective-permute-start | bytes 196616 | tf_op jit(solution)/shard_map/ppermute | solution.py:143
  168.0 6.0 %collective-permute-start.23 = (f16[128,256]{1,0:T(8,128)(2,1)S(1)}, f16[128,256]{1,0:T(8,128)(2,1)S(1)}, u32[]{:S(2)}, u32[]{:S(2)}) collective-permute-start(f16[128,256]{1,0:T(8,128)(2,1)S(1)} %slice_convert_fusion.1), channel_id=1, source_target_pairs={{0,4},{1,5},{2,6},{3,7},{4,0},{5,1},{6,2},{7,3},{8,12},{9,13},{10,... | collective-permute-start | bytes 196616 | tf_op jit(solution)/shard_map/ppermute | solution.py:143
  174.2 2.9 %collective-permute-done.15 = f16[128,256]{1,0:T(8,128)(2,1)S(1)} collective-permute-done((f16[128,256]{1,0:T(8,128)(2,1)S(1)}, f16[128,256]{1,0:T(8,128)(2,1)S(1)}, u32[]{:S(2)}, u32[]{:S(2)}) %collective-permute-start.15) | collective-permute-done | bytes 65568 | tf_op jit(solution)/shard_map/ppermute | solution.py:143
  178.0 4.4 %collective-permute-done.31 = f16[128,256]{1,0:T(8,128)(2,1)S(1)} collective-permute-done((f16[128,256]{1,0:T(8,128)(2,1)S(1)}, f16[128,256]{1,0:T(8,128)(2,1)S(1)}, u32[]{:S(2)}, u32[]{:S(2)}) %collective-permute-start.31) | collective-permute-done | bytes 65568 | tf_op jit(solution)/shard_map/ppermute | solution.py:143
  182.5 1.0 fusion.2
  (109 shorter events, 15.9 us)
Async XLA Ops:
  0.0 7.8 %copy-start = (f32[512]{0:T(512)S(1)}, f32[512]{0:T(512)}, u32[]{:S(2)}) copy-start(f32[512]{0:T(512)} %param.12) | copy-start | bytes 6148
  1.6 24.0 %collective-permute-start = (bf16[128,256]{1,0:T(8,128)(2,1)S(1)}, bf16[128,256]{1,0:T(8,128)(2,1)}, u32[]{:S(2)}, u32[]{:S(2)}) collective-permute-start(bf16[128,256]{1,0:T(8,128)(2,1)S(1)} %get-tuple-element.9), channel_id=1, source_target_pairs={{0,32},{8,24},{16,48},{24,8},{32,0},{40,56},{48,16},{56,40},{64,96... | collective-permute-start | bytes 196616 | tf_op jit(solution)/shard_map/ppermute | solution.py:137
  4.9 23.6 %collective-permute-start.8 = (bf16[128,256]{1,0:T(8,128)(2,1)S(1)}, bf16[128,256]{1,0:T(8,128)(2,1)}, u32[]{:S(2)}, u32[]{:S(2)}) collective-permute-start(bf16[128,256]{1,0:T(8,128)(2,1)S(1)} %get-tuple-element.14), channel_id=1, source_target_pairs={{0,32},{8,24},{16,48},{24,8},{32,0},{40,56},{48,16},{56,40},{64,96... | collective-permute-start | bytes 196616 | tf_op jit(solution)/shard_map/ppermute | solution.py:137
  4.9 24.6 %collective-permute-start.16 = (bf16[128,256]{1,0:T(8,128)(2,1)S(1)}, bf16[128,256]{1,0:T(8,128)(2,1)S(1)}, u32[]{:S(2)}, u32[]{:S(2)}) collective-permute-start(bf16[128,256]{1,0:T(8,128)(2,1)S(1)} %get-tuple-element.16), channel_id=1, source_target_pairs={{0,32},{8,24},{16,48},{24,8},{32,0},{40,56},{48,16},{56,40},{64,96... | collective-permute-start | bytes 196616 | tf_op jit(solution)/shard_map/ppermute | solution.py:137
  7.8 23.7 %collective-permute-start.24 = (bf16[128,256]{1,0:T(8,128)(2,1)S(1)}, bf16[128,256]{1,0:T(8,128)(2,1)S(1)}, u32[]{:S(2)}, u32[]{:S(2)}) collective-permute-start(bf16[128,256]{1,0:T(8,128)(2,1)S(1)} %get-tuple-element.15), channel_id=1, source_target_pairs={{0,32},{8,24},{16,48},{24,8},{32,0},{40,56},{48,16},{56,40},{64,96... | collective-permute-start | bytes 196616 | tf_op jit(solution)/shard_map/ppermute | solution.py:137
  24.0 48.5 %copy-start.10 = (f32[64]{0:T(128)S(1)}, f32[64]{0:T(128)}, u32[]{:S(2)}) copy-start(f32[64]{0:T(128)} %param.11) | copy-start | bytes 772
  26.4 7.6 %collective-permute-start.1 = (bf16[256,256]{1,0:T(8,128)(2,1)S(1)}, bf16[256,256]{1,0:T(8,128)(2,1)S(1)}, u32[]{:S(2)}, u32[]{:S(2)}) collective-permute-start(bf16[256,256]{1,0:T(8,128)(2,1)S(1)} %pad_maximum_fusion.8), channel_id=1, source_target_pairs={{0,16},{8,40},{16,0},{24,56},{32,48},{40,8},{48,32},{56,24},{64,80... | collective-permute-start | bytes 393224 | tf_op jit(solution)/shard_map/ppermute | solution.py:137
  29.3 7.5 %collective-permute-start.9 = (bf16[256,256]{1,0:T(8,128)(2,1)S(1)}, bf16[256,256]{1,0:T(8,128)(2,1)S(1)}, u32[]{:S(2)}, u32[]{:S(2)}) collective-permute-start(bf16[256,256]{1,0:T(8,128)(2,1)S(1)} %pad_maximum_fusion.9), channel_id=1, source_target_pairs={{0,16},{8,40},{16,0},{24,56},{32,48},{40,8},{48,32},{56,24},{64,80... | collective-permute-start | bytes 393224 | tf_op jit(solution)/shard_map/ppermute | solution.py:137
  29.5 9.1 %collective-permute-start.17 = (bf16[256,256]{1,0:T(8,128)(2,1)S(1)}, bf16[256,256]{1,0:T(8,128)(2,1)S(1)}, u32[]{:S(2)}, u32[]{:S(2)}) collective-permute-start(bf16[256,256]{1,0:T(8,128)(2,1)S(1)} %pad_maximum_fusion.10), channel_id=1, source_target_pairs={{0,16},{8,40},{16,0},{24,56},{32,48},{40,8},{48,32},{56,24},{64,80... | collective-permute-start | bytes 393224 | tf_op jit(solution)/shard_map/ppermute | solution.py:137
  31.5 8.5 %collective-permute-start.25 = (bf16[256,256]{1,0:T(8,128)(2,1)S(1)}, bf16[256,256]{1,0:T(8,128)(2,1)S(1)}, u32[]{:S(2)}, u32[]{:S(2)}) collective-permute-start(bf16[256,256]{1,0:T(8,128)(2,1)S(1)} %pad_maximum_fusion.11), channel_id=1, source_target_pairs={{0,16},{8,40},{16,0},{24,56},{32,48},{40,8},{48,32},{56,24},{64,80... | collective-permute-start | bytes 393224 | tf_op jit(solution)/shard_map/ppermute | solution.py:137
  34.9 6.9 %collective-permute-start.2 = (bf16[512,256]{1,0:T(8,128)(2,1)S(1)}, bf16[512,256]{1,0:T(8,128)(2,1)S(1)}, u32[]{:S(2)}, u32[]{:S(2)}) collective-permute-start(bf16[512,256]{1,0:T(8,128)(2,1)S(1)} %pad_maximum_fusion.4), channel_id=1, source_target_pairs={{0,64},{8,200},{16,80},{24,216},{32,96},{40,232},{48,112},{56,248}... | collective-permute-start | bytes 786440 | tf_op jit(solution)/shard_map/ppermute | solution.py:137
  37.7 7.0 %collective-permute-start.10 = (bf16[512,256]{1,0:T(8,128)(2,1)S(1)}, bf16[512,256]{1,0:T(8,128)(2,1)S(1)}, u32[]{:S(2)}, u32[]{:S(2)}) collective-permute-start(bf16[512,256]{1,0:T(8,128)(2,1)S(1)} %pad_maximum_fusion.5), channel_id=1, source_target_pairs={{0,64},{8,200},{16,80},{24,216},{32,96},{40,232},{48,112},{56,248}... | collective-permute-start | bytes 786440 | tf_op jit(solution)/shard_map/ppermute | solution.py:137
  38.6 11.1 %collective-permute-start.18 = (bf16[512,256]{1,0:T(8,128)(2,1)S(1)}, bf16[512,256]{1,0:T(8,128)(2,1)S(1)}, u32[]{:S(2)}, u32[]{:S(2)}) collective-permute-start(bf16[512,256]{1,0:T(8,128)(2,1)S(1)} %pad_maximum_fusion.6), channel_id=1, source_target_pairs={{0,64},{8,200},{16,80},{24,216},{32,96},{40,232},{48,112},{56,248}... | collective-permute-start | bytes 786440 | tf_op jit(solution)/shard_map/ppermute | solution.py:137
  40.0 15.2 %collective-permute-start.26 = (bf16[512,256]{1,0:T(8,128)(2,1)S(1)}, bf16[512,256]{1,0:T(8,128)(2,1)S(1)}, u32[]{:S(2)}, u32[]{:S(2)}) collective-permute-start(bf16[512,256]{1,0:T(8,128)(2,1)S(1)} %pad_maximum_fusion.7), channel_id=1, source_target_pairs={{0,64},{8,200},{16,80},{24,216},{32,96},{40,232},{48,112},{56,248}... | collective-permute-start | bytes 786440 | tf_op jit(solution)/shard_map/ppermute | solution.py:137
  42.7 16.0 %collective-permute-start.3 = (bf16[1024,256]{1,0:T(8,128)(2,1)S(1)}, bf16[1024,256]{1,0:T(8,128)(2,1)S(1)}, u32[]{:S(2)}, u32[]{:S(2)}) collective-permute-start(bf16[1024,256]{1,0:T(8,128)(2,1)S(1)} %pad_maximum_fusion), channel_id=1, source_target_pairs={{0,192},{8,72},{16,208},{24,88},{32,224},{40,104},{48,240},{56,120... | collective-permute-start | bytes 1572872 | tf_op jit(solution)/shard_map/ppermute | solution.py:137
  45.6 13.9 %collective-permute-start.11 = (bf16[1024,256]{1,0:T(8,128)(2,1)S(1)}, bf16[1024,256]{1,0:T(8,128)(2,1)S(1)}, u32[]{:S(2)}, u32[]{:S(2)}) collective-permute-start(bf16[1024,256]{1,0:T(8,128)(2,1)S(1)} %pad_maximum_fusion.1), channel_id=1, source_target_pairs={{0,192},{8,72},{16,208},{24,88},{32,224},{40,104},{48,240},{56,120... | collective-permute-start | bytes 1572872 | tf_op jit(solution)/shard_map/ppermute | solution.py:137
  49.7 14.1 %collective-permute-start.19 = (bf16[1024,256]{1,0:T(8,128)(2,1)S(1)}, bf16[1024,256]{1,0:T(8,128)(2,1)S(1)}, u32[]{:S(2)}, u32[]{:S(2)}) collective-permute-start(bf16[1024,256]{1,0:T(8,128)(2,1)S(1)} %pad_maximum_fusion.2), channel_id=1, source_target_pairs={{0,192},{8,72},{16,208},{24,88},{32,224},{40,104},{48,240},{56,120... | collective-permute-start | bytes 1572872 | tf_op jit(solution)/shard_map/ppermute | solution.py:137
  55.3 14.1 %collective-permute-start.27 = (bf16[1024,256]{1,0:T(8,128)(2,1)S(1)}, bf16[1024,256]{1,0:T(8,128)(2,1)S(1)}, u32[]{:S(2)}, u32[]{:S(2)}) collective-permute-start(bf16[1024,256]{1,0:T(8,128)(2,1)S(1)} %pad_maximum_fusion.3), channel_id=1, source_target_pairs={{0,192},{8,72},{16,208},{24,88},{32,224},{40,104},{48,240},{56,120... | collective-permute-start | bytes 1572872 | tf_op jit(solution)/shard_map/ppermute | solution.py:137
  59.5 15.8 %collective-permute-start.4 = (bf16[2048,256]{1,0:T(8,128)(2,1)}, bf16[2048,256]{1,0:T(8,128)(2,1)}, u32[]{:S(2)}, u32[]{:S(2)}) collective-permute-start(bf16[2048,256]{1,0:T(8,128)(2,1)} %constant_dynamic-update-slice_fusion.mine), channel_id=1, source_target_pairs={{0,8},{8,0},{16,24},{24,16},{32,40},{40,32},{48,56},{56,48},{64,72... | collective-permute-start | bytes 3145736 | tf_op jit(solution)/shard_map/ppermute | solution.py:138
  59.5 23.9 %copy-start.3 = (bf16[2048,256]{1,0:T(8,128)(2,1)}, bf16[2048,256]{1,0:T(8,128)(2,1)S(1)}, u32[]{:S(2)}) copy-start(bf16[2048,256]{1,0:T(8,128)(2,1)S(1)} %constant_dynamic-update-slice_fusion.5.mine) | copy-start | bytes 3145732
  59.6 27.2 %collective-permute-start.12 = (bf16[2048,256]{1,0:T(8,128)(2,1)S(1)}, bf16[2048,256]{1,0:T(8,128)(2,1)}, u32[]{:S(2)}, u32[]{:S(2)}) collective-permute-start(bf16[2048,256]{1,0:T(8,128)(2,1)S(1)} %constant_dynamic-update-slice_fusion.5.mine), channel_id=1, source_target_pairs={{0,8},{8,0},{16,24},{24,16},{32,40},{40,32},{48,56},{56,48},{64,72... | collective-permute-start | bytes 3145736 | tf_op jit(solution)/shard_map/ppermute | solution.py:138
  63.8 21.5 %copy-start.2 = (bf16[2048,256]{1,0:T(8,128)(2,1)}, bf16[2048,256]{1,0:T(8,128)(2,1)S(1)}, u32[]{:S(2)}) copy-start(bf16[2048,256]{1,0:T(8,128)(2,1)S(1)} %constant_dynamic-update-slice_fusion.10.mine) | copy-start | bytes 3145732
  63.8 32.9 %collective-permute-start.20 = (bf16[2048,256]{1,0:T(8,128)(2,1)S(1)}, bf16[2048,256]{1,0:T(8,128)(2,1)}, u32[]{:S(2)}, u32[]{:S(2)}) collective-permute-start(bf16[2048,256]{1,0:T(8,128)(2,1)S(1)} %constant_dynamic-update-slice_fusion.10.mine), channel_id=1, source_target_pairs={{0,8},{8,0},{16,24},{24,16},{32,40},{40,32},{48,56},{56,48},{64,72... | collective-permute-start | bytes 3145736 | tf_op jit(solution)/shard_map/ppermute | solution.py:138
  69.4 25.5 %copy-start.1 = (bf16[2048,256]{1,0:T(8,128)(2,1)}, bf16[2048,256]{1,0:T(8,128)(2,1)S(1)}, u32[]{:S(2)}) copy-start(bf16[2048,256]{1,0:T(8,128)(2,1)S(1)} %constant_dynamic-update-slice_fusion.15.mine) | copy-start | bytes 3145732
  69.4 38.1 %collective-permute-start.28 = (bf16[2048,256]{1,0:T(8,128)(2,1)S(1)}, bf16[2048,256]{1,0:T(8,128)(2,1)}, u32[]{:S(2)}, u32[]{:S(2)}) collective-permute-start(bf16[2048,256]{1,0:T(8,128)(2,1)S(1)} %constant_dynamic-update-slice_fusion.15.mine), channel_id=1, source_target_pairs={{0,8},{8,0},{16,24},{24,16},{32,40},{40,32},{48,56},{56,48},{64,72... | collective-permute-start | bytes 3145736 | tf_op jit(solution)/shard_map/ppermute | solution.py:138
  85.3 65.1 %collective-permute-start.5 = (f16[512,256]{1,0:T(8,128)(2,1)}, f16[512,256]{1,0:T(8,128)(2,1)}, u32[]{:S(2)}, u32[]{:S(2)}) collective-permute-start(f16[512,256]{1,0:T(8,128)(2,1)} %convert_element_type.64), channel_id=1, source_target_pairs={{0,1},{1,0},{2,3},{3,2},{4,5},{5,4},{6,7},{7,6},{8,11},{9,10},{10,... | collective-permute-start | bytes 786440 | tf_op jit(solution)/shard_map/ppermute | solution.py:143
  96.0 58.5 %collective-permute-start.13 = (f16[512,256]{1,0:T(8,128)(2,1)S(1)}, f16[512,256]{1,0:T(8,128)(2,1)S(1)}, u32[]{:S(2)}, u32[]{:S(2)}) collective-permute-start(f16[512,256]{1,0:T(8,128)(2,1)S(1)} %convert_element_type.69), channel_id=1, source_target_pairs={{0,1},{1,0},{2,3},{3,2},{4,5},{5,4},{6,7},{7,6},{8,11},{9,10},{10,... | collective-permute-start | bytes 786440 | tf_op jit(solution)/shard_map/ppermute | solution.py:143
  105.9 49.3 %collective-permute-start.21 = (f16[512,256]{1,0:T(8,128)(2,1)S(1)}, f16[512,256]{1,0:T(8,128)(2,1)}, u32[]{:S(2)}, u32[]{:S(2)}) collective-permute-start(f16[512,256]{1,0:T(8,128)(2,1)S(1)} %convert_element_type.74), channel_id=1, source_target_pairs={{0,1},{1,0},{2,3},{3,2},{4,5},{5,4},{6,7},{7,6},{8,11},{9,10},{10,... | collective-permute-start | bytes 786440 | tf_op jit(solution)/shard_map/ppermute | solution.py:143
  116.8 42.3 %collective-permute-start.29 = (f16[512,256]{1,0:T(8,128)(2,1)S(1)}, f16[512,256]{1,0:T(8,128)(2,1)S(1)}, u32[]{:S(2)}, u32[]{:S(2)}) collective-permute-start(f16[512,256]{1,0:T(8,128)(2,1)S(1)} %convert_element_type.79), channel_id=1, source_target_pairs={{0,1},{1,0},{2,3},{3,2},{4,5},{5,4},{6,7},{7,6},{8,11},{9,10},{10,... | collective-permute-start | bytes 786440 | tf_op jit(solution)/shard_map/ppermute | solution.py:143
  142.0 9.5 %copy-start.7 = (f32[512,256]{1,0:T(8,128)S(1)}, f32[512,256]{1,0:T(8,128)}, u32[]{:S(2)}) copy-start(f32[512,256]{1,0:T(8,128)} %mm.8) | copy-start | bytes 1572868
  142.0 12.6 %copy-start.6 = (f32[512,256]{1,0:T(8,128)S(1)}, f32[512,256]{1,0:T(8,128)}, u32[]{:S(2)}) copy-start(f32[512,256]{1,0:T(8,128)} %mm.10) | copy-start | bytes 1572868
  142.0 14.2 %copy-start.5 = (f32[512,256]{1,0:T(8,128)S(1)}, f32[512,256]{1,0:T(8,128)}, u32[]{:S(2)}) copy-start(f32[512,256]{1,0:T(8,128)} %mm.12) | copy-start | bytes 1572868
  150.3 23.7 %copy-start.4 = (f32[512,256]{1,0:T(8,128)S(1)}, f32[512,256]{1,0:T(8,128)}, u32[]{:S(2)}) copy-start(f32[512,256]{1,0:T(8,128)} %mm.14) | copy-start | bytes 1572868
  150.3 32.1 %copy-start.8 = (f32[128,1024]{1,0:T(8,128)S(1)}, f32[128,1024]{1,0:T(8,128)}, u32[]{:S(2)}) copy-start(f32[128,1024]{1,0:T(8,128)} %param.10) | copy-start | bytes 1572868
  150.4 32.1 %copy-start.9 = (f32[1024]{0:T(1024)S(1)}, f32[1024]{0:T(1024)}, u32[]{:S(2)}) copy-start(f32[1024]{0:T(1024)} %param.13) | copy-start | bytes 12292
  151.5 9.2 %collective-permute-start.6 = (f16[256,256]{1,0:T(8,128)(2,1)S(1)}, f16[256,256]{1,0:T(8,128)(2,1)S(1)}, u32[]{:S(2)}, u32[]{:S(2)}) collective-permute-start(f16[256,256]{1,0:T(8,128)(2,1)S(1)} %fusion.10), channel_id=1, source_target_pairs={{0,3},{1,2},{2,1},{3,0},{4,7},{5,6},{6,5},{7,4},{8,9},{9,8},{10,11... | collective-permute-start | bytes 393224 | tf_op jit(solution)/shard_map/ppermute | solution.py:143
  154.7 13.1 %collective-permute-start.14 = (f16[256,256]{1,0:T(8,128)(2,1)S(1)}, f16[256,256]{1,0:T(8,128)(2,1)S(1)}, u32[]{:S(2)}, u32[]{:S(2)}) collective-permute-start(f16[256,256]{1,0:T(8,128)(2,1)S(1)} %fusion.8), channel_id=1, source_target_pairs={{0,3},{1,2},{2,1},{3,0},{4,7},{5,6},{6,5},{7,4},{8,9},{9,8},{10,11... | collective-permute-start | bytes 393224 | tf_op jit(solution)/shard_map/ppermute | solution.py:143
  156.3 11.6 %collective-permute-start.22 = (f16[256,256]{1,0:T(8,128)(2,1)S(1)}, f16[256,256]{1,0:T(8,128)(2,1)S(1)}, u32[]{:S(2)}, u32[]{:S(2)}) collective-permute-start(f16[256,256]{1,0:T(8,128)(2,1)S(1)} %fusion.6), channel_id=1, source_target_pairs={{0,3},{1,2},{2,1},{3,0},{4,7},{5,6},{6,5},{7,4},{8,9},{9,8},{10,11... | collective-permute-start | bytes 393224 | tf_op jit(solution)/shard_map/ppermute | solution.py:143
  160.2 13.8 %collective-permute-start.30 = (f16[256,256]{1,0:T(8,128)(2,1)S(1)}, f16[256,256]{1,0:T(8,128)(2,1)S(1)}, u32[]{:S(2)}, u32[]{:S(2)}) collective-permute-start(f16[256,256]{1,0:T(8,128)(2,1)S(1)} %fusion.4), channel_id=1, source_target_pairs={{0,3},{1,2},{2,1},{3,0},{4,7},{5,6},{6,5},{7,4},{8,9},{9,8},{10,11... | collective-permute-start | bytes 393224 | tf_op jit(solution)/shard_map/ppermute | solution.py:143
  160.8 13.4 %collective-permute-start.7 = (f16[128,256]{1,0:T(8,128)(2,1)S(1)}, f16[128,256]{1,0:T(8,128)(2,1)S(1)}, u32[]{:S(2)}, u32[]{:S(2)}) collective-permute-start(f16[128,256]{1,0:T(8,128)(2,1)S(1)} %slice_convert_fusion.3), channel_id=1, source_target_pairs={{0,4},{1,5},{2,6},{3,7},{4,0},{5,1},{6,2},{7,3},{8,12},{9,13},{10,... | collective-permute-start | bytes 196616 | tf_op jit(solution)/shard_map/ppermute | solution.py:143
  167.8 9.3 %collective-permute-start.15 = (f16[128,256]{1,0:T(8,128)(2,1)S(1)}, f16[128,256]{1,0:T(8,128)(2,1)S(1)}, u32[]{:S(2)}, u32[]{:S(2)}) collective-permute-start(f16[128,256]{1,0:T(8,128)(2,1)S(1)} %slice_convert_fusion.2), channel_id=1, source_target_pairs={{0,4},{1,5},{2,6},{3,7},{4,0},{5,1},{6,2},{7,3},{8,12},{9,13},{10,... | collective-permute-start | bytes 196616 | tf_op jit(solution)/shard_map/ppermute | solution.py:143
  168.0 9.9 %collective-permute-start.23 = (f16[128,256]{1,0:T(8,128)(2,1)S(1)}, f16[128,256]{1,0:T(8,128)(2,1)S(1)}, u32[]{:S(2)}, u32[]{:S(2)}) collective-permute-start(f16[128,256]{1,0:T(8,128)(2,1)S(1)} %slice_convert_fusion.1), channel_id=1, source_target_pairs={{0,4},{1,5},{2,6},{3,7},{4,0},{5,1},{6,2},{7,3},{8,12},{9,13},{10,... | collective-permute-start | bytes 196616 | tf_op jit(solution)/shard_map/ppermute | solution.py:143
  174.1 8.3 %collective-permute-start.31 = (f16[128,256]{1,0:T(8,128)(2,1)S(1)}, f16[128,256]{1,0:T(8,128)(2,1)S(1)}, u32[]{:S(2)}, u32[]{:S(2)}) collective-permute-start(f16[128,256]{1,0:T(8,128)(2,1)S(1)} %slice_convert_fusion), channel_id=1, source_target_pairs={{0,4},{1,5},{2,6},{3,7},{4,0},{5,1},{6,2},{7,3},{8,12},{9,13},{10,... | collective-permute-start | bytes 196616 | tf_op jit(solution)/shard_map/ppermute | solution.py:143

commit v2 on v0

v2 whole, which is shorter than its diff:
```python
import functools

import jax
import jax.numpy as jnp
from jax import lax
from jax.experimental import pallas as pl
from jax.experimental.pallas import tpu as pltpu
from jax.sharding import PartitionSpec as P

VIRT = 512
ROWS, COLS = 32, 8
F8 = jnp.float8_e4m3fn
CHUNKS = (256, 384, 384)
FAR = ((0,), (1,), (2,))
GATHER = ((2 << 1, 1 << 1), (1 << 1, 2 << 1), (1 << 3, 3 << 3), (3 << 3, 1 << 3))
REDUCE = ((1, 3), (3, 1))
SCALE = 8.0
LO = 2.0**17
A8 = 64.0
PREP_LIMIT = 56
MM_LIMIT = 32


def row_perm(step):
    return [(r, r ^ step[r & 1]) for r in range(ROWS)]


def all_perm(step):
    pairs = []
    for r in range(ROWS):
        for c in range(COLS):
            pairs.append((r * COLS + c, r * COLS + (c ^ step[r & 1])))
    return pairs


def bits(value):
    return value & 1, (value >> 1) & 1


def piece_at(piece, row):
    core = piece & 1
    z0, z1 = bits((piece ^ row) >> 1)
    y0, y1 = bits((piece ^ row) >> 3)
    first, second = z1 + 2 * z0, z0 + 2 * z1
    turn, walk = (y0 ^ y1) * 4 + y1 * 8, y1 * 4 + (y0 ^ y1) * 8
    place = jnp.where(core == 0, first + turn, second + walk)
    return place + ((piece ^ row) & 1) * 16


def tile_at(dest, row, col):
    x0, x1 = bits((dest ^ col) & 3)
    even = (x0 ^ x1) * 2 + x1
    odd = x1 * 2 + (x0 ^ x1)
    return jnp.where((row & 1) == 0, even, odd)


VMEM = pl.BlockSpec(memory_space=pltpu.VMEM)
ANY = pl.BlockSpec(memory_space=pl.ANY)


def prep_kernel(occ, x_hbm, *refs):
    hi_hbm, lo_hbm, x_ref, hi_ref, lo_ref, in_sems, out_sems = refs[2 * occ :]
    row, col = lax.axis_index("row"), lax.axis_index("col")
    depth = x_hbm.shape[1]
    side = VIRT // 4
    count = depth // VIRT
    loads = []
    for j in range(count):
        span = pl.ds(j * VIRT, VIRT)
        part = x_hbm.at[pl.ds(occ * VIRT, VIRT), span]
        loads.append(pltpu.make_async_copy(part, x_ref.at[:, span], in_sems.at[j]))
        loads[-1].start()
    stores = []
    for g in range(count):
        loads[g].wait()
        x = x_ref[:, g * VIRT : (g + 1) * VIRT]
        both = (x.astype(jnp.float32) + x.T.astype(jnp.float32)) * SCALE
        hi = both.astype(jnp.bfloat16)
        lo = ((both - hi.astype(jnp.float32)) * LO).astype(F8)
        for u in range(4):
            over = pl.ds(pl.multiple_of(piece_at(g * 4 + u, row) * side, side), side)
            for s in range(4):
                down = pl.ds(pl.multiple_of(tile_at(s, row, col) * side, side), side)
                part = (slice(s * side, (s + 1) * side), slice(u * side, (u + 1) * side))
                hi_ref[down, over] = hi[part]
                lo_ref[down, over] = lo[part]
            for n, (src, dst) in enumerate(((hi_ref, hi_hbm), (lo_ref, lo_hbm))):
                sem = out_sems.at[n, g * 4 + u]
                to = dst.at[occ, :, over]
                stores.append(pltpu.make_async_copy(src.at[:, over], to, sem))
                stores[-1].start()
    for store in stores:
        store.wait()


def prep(integrals, occ, old=()):
    depth = integrals.shape[1]
    hi = jax.ShapeDtypeStruct((10, VIRT, depth), jnp.bfloat16)
    lo = jax.ShapeDtypeStruct((18, VIRT, depth), F8)
    return pl.pallas_call(
        functools.partial(prep_kernel, occ),
        in_specs=[ANY] * (1 + len(old)),
        out_specs=[ANY, ANY],
        out_shape=[hi, lo],
        scratch_shapes=[
            pltpu.VMEM((VIRT, depth), jnp.bfloat16),
            pltpu.VMEM((VIRT, depth), hi.dtype),
            pltpu.VMEM((VIRT, depth), lo.dtype),
            pltpu.SemaphoreType.DMA((depth // VIRT,)),
            pltpu.SemaphoreType.DMA((2, ROWS)),
        ],
        input_output_aliases={1 + n: n for n in range(len(old))},
        compiler_params=pltpu.CompilerParams(vmem_limit_bytes=PREP_LIMIT << 20),
        cost_estimate=pl.CostEstimate(
            flops=0, bytes_accessed=VIRT * depth * 10, transcendentals=0
        ),
        name="prep",
    )(integrals, *old)


def base_kernel(vir, occ, out):
    place = lax.axis_index("row") * COLS + lax.axis_index("col")
    per_occ = vir.shape[0]
    out[...] = vir[pl.ds(place % per_occ, 1), :] - occ[place // per_occ]


def base(vir_energy, occ_energy, out_rows):
    return pl.pallas_call(
        base_kernel,
        in_specs=[VMEM, pl.BlockSpec(memory_space=pltpu.SMEM)],
        out_specs=VMEM,
        out_shape=jax.ShapeDtypeStruct((1, out_rows), jnp.float32),
        compiler_params=pltpu.CompilerParams(vmem_limit_bytes=1 << 20),
        name="base",
    )(vir_energy.reshape(-1, out_rows), occ_energy)


def mm_kernel(spans, hi_hbm, lo_hbm, *refs):
    count = len(spans)
    pieces, (send, keep, hi, lo, sems) = refs[:count], refs[count:]
    depth = pieces[0].shape[0]
    side = VIRT // 4
    last = count - 1

    def copies(i, k):
        span = pl.ds(spans[k], depth)
        return [
            pltpu.make_async_copy(src.at[i, :, span], dst.at[k], sems.at[k, m])
            for m, (src, dst) in enumerate(((hi_hbm, hi), (lo_hbm, lo)))
        ]

    def begin(i, k):
        for copy in copies(i, k):
            copy.start()

    for k in range(last):
        begin(0, k)
    values = [piece[...] for piece in pieces]
    small = [(value.astype(jnp.float32) * A8).astype(F8) for value in values]

    @pl.loop(0, 2)
    def _(i):
        total = None
        for k in range(count):
            for copy in copies(i, k):
                copy.wait()
            if k == 0:
                begin(i, last)
            else:
                pl.when(i == 0)(functools.partial(begin, 1, k - 1))
            part = jnp.dot(hi[k], values[k], preferred_element_type=jnp.float32)
            rest = jnp.dot(lo[k], small[k], preferred_element_type=jnp.float32)
            part = part + rest * (1.0 / (LO * A8))
            total = part if k == 0 else total + part
        for q in range(4):
            (keep, send)[q // 2][q % 2, i] = total[q * side : (q + 1) * side]


def mm(tops, spans, pieces):
    depth, cols = pieces[0].shape
    count = len(spans)
    out = jax.ShapeDtypeStruct((2, 2, VIRT // 4, cols), jnp.float32)
    return pl.pallas_call(
        functools.partial(mm_kernel, spans),
        in_specs=[ANY] * 2 + [VMEM] * count,
        out_specs=[VMEM] * 2,
        out_shape=[out] * 2,
        scratch_shapes=[
            pltpu.VMEM((count, VIRT, depth), jnp.bfloat16),
            pltpu.VMEM((count, VIRT, depth), F8),
            pltpu.SemaphoreType.DMA((count, 2)),
        ],
        compiler_params=pltpu.CompilerParams(vmem_limit_bytes=MM_LIMIT << 20),
        cost_estimate=pl.CostEstimate(
            flops=6 * VIRT * 2 * depth * cols * count,
            bytes_accessed=6 * count * VIRT * depth,
            transcendentals=0,
        ),
        name="mm",
    )(*tops, *pieces)


def gather(block):
    for n, step in enumerate(GATHER):
        got = lax.ppermute(block, "row", row_perm(step))
        if n < 3:
            block = jnp.concatenate([block, got], axis=0)
    other = lax.ppermute(block, "row", row_perm((1, 1)))
    late = lax.ppermute(got, "row", row_perm((1, 1)))
    return (block, other), (got, late)


def swap(value, step):
    sent = value.astype(jnp.float16)
    got = lax.ppermute(sent, ("row", "col"), all_perm(step))
    return got.astype(jnp.float32)


def body(integrals, amplitudes, source, occ_energy, vir_energy, col_energy):
    col = lax.axis_index("col")
    out_rows = source.shape[0]
    tops = ()
    for occ in range(2):
        tops = prep(integrals, occ, tuple(tops))
    below = base(vir_energy, occ_energy, out_rows)[0]
    halves = []
    start = 0
    for width in CHUNKS:
        early, late = gather(amplitudes[:, start : start + width])
        depth = early[0].shape[0]
        send, keep = mm(tops, (0, 2 * depth, depth, 3 * depth), early + late)
        keep = keep + swap(send, REDUCE[0])
        keep = keep[0] + swap(keep[1], REDUCE[1])
        near = lax.dynamic_index_in_dim(keep, col // 4, 0, keepdims=False)
        far = lax.dynamic_index_in_dim(keep, 1 - col // 4, 0, keepdims=False)
        halves.append((near, far))
        start += width
    done = []
    for group in FAR:
        near, far = (jnp.concatenate([halves[n][m] for n in group], axis=1) for m in range(2))
        done.append(near + swap(far, (4, 4)))
    summed = jnp.concatenate(done, axis=1) * (1.0 / SCALE)
    denom = below[:, None] + col_energy[None, :]
    return -(source + summed) / denom


def solution(mesh):
    in_specs = (P("row", "col"), P(("col", "row"), None), P(("row", "col"), None), P(), P(), P())
    out_specs = P(("row", "col"), None)
    return jax.shard_map(body, mesh=mesh, in_specs=in_specs, out_specs=out_specs, check_vma=False)
```

time: 236 us -> 128 us (0.54)
  waiting for transfers between devices: 163 us -> 30.8 us
  starting transfers between devices: 0.04 us -> 51.4 us
  Pallas kernels: 0 us -> 38 us
  local copies, waits for them, and re-layouts: 33.4 us -> 2.62 us
  matrix products: 23.1 us -> 0 us
  between operations: 13.5 us -> 0.32 us
    reduce_scatter x1 -> x0, waiting for transfers between devices: 122 us -> none  [per_device(): lax.psum_scatter(both_rows(jnp.int32(0), lax.axis_size('col') * out_rows)...]
    ppermute x0 -> x27, starting transfers between devices: none -> 51.4 us  [the longest x9 27.8 us: swap(): got = lax.ppermute(sent, ('row', 'col'), all_perm(step))]
    all_gather x1 -> x0, waiting for transfers between devices: 40 us -> none  [per_device(): gathered = lax.all_gather(amplitudes, 'row', axis=0, tiled=True)]
    pallas_call x0 -> x6, Pallas kernels: none -> 38 us  [the longest x3 26.2 us: mm(): pl.pallas_call(functools.partial(mm_kernel, spans), in_specs=[ANY] * 2 +...]
    ppermute x0 -> x27, waiting for transfers between devices: none -> 30.8 us  [the longest x9 15.5 us: swap(): got = lax.ppermute(sent, ('row', 'col'), all_perm(step))]
    dot_general x2 -> x0, matrix products: 23.1 us -> none  [the longest x1 12.7 us: both_rows(): jnp.dot(integrals, gathered, preferred_element_type=jnp.float32)]
    dot_general x2 -> x0, local copies, waits for them, and re-layouts: 21.1 us -> none  [summed_terms(): lax.dot_general(blocks, amp_blocks, (((1, 2), (1, 0)), ((), ())), preferr...]
    unnamed x17 -> x10, local copies, waits for them, and re-layouts: 12.4 us -> 0.81 us
  transfers between devices with their start and end apart: 2 -> 27, of which waited for: 2 -> 11; matrix products, arithmetic and copies ran while one was open for 14% -> 2% of each run, Pallas kernels for 0% -> 30%
where the time goes in v2:
time: 128 us; the launch traced here: 126 us
  starting transfers between devices  51.4 us (40%)
  Pallas kernels  38 us (30%)
  waiting for transfers between devices  30.8 us (24%)
  other arithmetic  2.96 us (2%)
  local copies, waits for them, and re-layouts  2.62 us (2%)
    ppermute x9, starting transfers between devices, swap(): got = lax.ppermute(sent, ('row', 'col'), all_perm(step))  27.8 us
    pallas_call x3, Pallas kernels, mm(): pl.pallas_call(functools.partial(mm_kernel, spans), in_specs=[ANY] * 2 +...  26.2 us
    ppermute x12, starting transfers between devices, gather(): got = lax.ppermute(block, 'row', row_perm(step))  19.1 us
    ppermute x9, waiting for transfers between devices, swap(): got = lax.ppermute(sent, ('row', 'col'), all_perm(step))  15.5 us
    ppermute x12, waiting for transfers between devices, gather(): got = lax.ppermute(block, 'row', row_perm(step))  15.3 us
    pallas_call x2, Pallas kernels, prep(): pl.pallas_call(functools.partial(prep_kernel, occ), in_specs=[ANY] * (1 +...  11.3 us
    ppermute x3, starting transfers between devices, gather(): other = lax.ppermute(block, 'row', row_perm((1, 1)))  3.55 us
  transfers between devices with their start and end apart: 27, of which 11 were waited for; matrix products, arithmetic and copies ran while one was open for 2% of the time, Pallas kernels for 30%

profile of v2, /device:TPU:8, one launch (start us, length us, event | category | flops | bytes accessed | tf_op | source)
XLA Modules:
  0.0 126.1 jit_solution(14325470622728951727)
XLA Ops:
  0.0 0.8 slice.30
  0.8 3.3 %collective-permute-start = (bf16[128,256]{1,0:T(8,128)(2,1)S(1)}, bf16[128,256]{1,0:T(8,128)(2,1)S(1)}, u32[]{:S(2)}, u32[]{:S(2)}) collective-permute-start(bf16[128,256]{1,0:T(8,128)(2,1)S(1)} %slice.30), channel_id=1, source_target_pairs={{0,32},{8,24},{16,48},{24,8},{32,0},{40,56},{48,16},{56,40},{64,96... | collective-permute-start | bytes 196616 | tf_op jit(solution)/shard_map/ppermute | solution.py:205
  4.1 2.2 %collective-permute-done = bf16[128,256]{1,0:T(8,128)(2,1)S(1)} collective-permute-done((bf16[128,256]{1,0:T(8,128)(2,1)S(1)}, bf16[128,256]{1,0:T(8,128)(2,1)S(1)}, u32[]{:S(2)}, u32[]{:S(2)}) %collective-permute-start) | collective-permute-done | bytes 65568 | tf_op jit(solution)/shard_map/ppermute | solution.py:205
  6.4 2.0 %collective-permute-start.1 = (bf16[256,256]{1,0:T(8,128)(2,1)S(1)}, bf16[256,256]{1,0:T(8,128)(2,1)S(1)}, u32[]{:S(2)}, u32[]{:S(2)}) collective-permute-start(bf16[256,256]{1,0:T(8,128)(2,1)S(1)} %pad_maximum_fusion.8), channel_id=1, source_target_pairs={{0,16},{8,40},{16,0},{24,56},{32,48},{40,8},{48,32},{56,24},{64,80... | collective-permute-start | bytes 393224 | tf_op jit(solution)/shard_map/ppermute | solution.py:205
  8.4 3.2 %collective-permute-done.1 = bf16[256,256]{1,0:T(8,128)(2,1)S(1)} collective-permute-done((bf16[256,256]{1,0:T(8,128)(2,1)S(1)}, bf16[256,256]{1,0:T(8,128)(2,1)S(1)}, u32[]{:S(2)}, u32[]{:S(2)}) %collective-permute-start.1) | collective-permute-done | bytes 131104 | tf_op jit(solution)/shard_map/ppermute | solution.py:205
  11.6 2.7 %collective-permute-start.2 = (bf16[512,256]{1,0:T(8,128)(2,1)S(1)}, bf16[512,256]{1,0:T(8,128)(2,1)S(1)}, u32[]{:S(2)}, u32[]{:S(2)}) collective-permute-start(bf16[512,256]{1,0:T(8,128)(2,1)S(1)} %pad_maximum_fusion.5), channel_id=1, source_target_pairs={{0,64},{8,200},{16,80},{24,216},{32,96},{40,232},{48,112},{56,248}... | collective-permute-start | bytes 786440 | tf_op jit(solution)/shard_map/ppermute | solution.py:205
  14.3 1.0 fusion.12
  15.2 0.9 collective-permute-start.18
  16.1 2.5 %collective-permute-done.2 = bf16[512,256]{1,0:T(8,128)(2,1)S(1)} collective-permute-done((bf16[512,256]{1,0:T(8,128)(2,1)S(1)}, bf16[512,256]{1,0:T(8,128)(2,1)S(1)}, u32[]{:S(2)}, u32[]{:S(2)}) %collective-permute-start.2) | collective-permute-done | bytes 262176 | tf_op jit(solution)/shard_map/ppermute | solution.py:205
  18.6 1.1 collective-permute-start.4
  19.7 1.6 %collective-permute-done.18 = bf16[128,384]{1,0:T(8,128)(2,1)S(1)} collective-permute-done((bf16[128,384]{1,0:T(8,128)(2,1)S(1)}, bf16[128,384]{1,0:T(8,128)(2,1)S(1)}, u32[]{:S(2)}, u32[]{:S(2)}) %collective-permute-start.18) | collective-permute-done | bytes 98336 | tf_op jit(solution)/shard_map/ppermute | solution.py:205
  21.3 0.3 collective-permute-start.19
  21.6 3.2 %collective-permute-start.9 = (bf16[128,384]{1,0:T(8,128)(2,1)S(1)}, bf16[128,384]{1,0:T(8,128)(2,1)S(1)}, u32[]{:S(2)}, u32[]{:S(2)}) collective-permute-start(bf16[128,384]{1,0:T(8,128)(2,1)S(1)} %get-tuple-element.25), channel_id=1, source_target_pairs={{0,32},{8,24},{16,48},{24,8},{32,0},{40,56},{48,16},{56,40},{64,96... | collective-permute-start | bytes 294920 | tf_op jit(solution)/shard_map/ppermute | solution.py:205
  24.8 4.1 %collective-permute-done.19 = bf16[256,384]{1,0:T(8,128)(2,1)S(1)} collective-permute-done((bf16[256,384]{1,0:T(8,128)(2,1)S(1)}, bf16[256,384]{1,0:T(8,128)(2,1)S(1)}, u32[]{:S(2)}, u32[]{:S(2)}) %collective-permute-start.19) | collective-permute-done | bytes 196640 | tf_op jit(solution)/shard_map/ppermute | solution.py:205
  28.9 1.2 collective-permute-start.20
  30.1 0.5 collective-permute-start.5
  30.6 0.3 collective-permute-start.10
  30.9 5.6 %prep.2 = (bf16[10,512,4096]{2,1,0:T(8,128)(2,1)}, f8e4m3fn[18,512,4096]{2,1,0:T(32,128)(4,1)}) custom-call(bf16[1024,4096]{1,0:T(8,128)(2,1)} %x_hbm.3), custom_call_target="tpu_custom_call" | custom-call | bytes 20971520 | tf_op jit(solution)/shard_map/prep/pallas_call | solution.py:100
  36.5 5.6 %prep.3 = (bf16[10,512,4096]{2,1,0:T(8,128)(2,1)}, f8e4m3fn[18,512,4096]{2,1,0:T(32,128)(4,1)}) custom-call(bf16[1024,4096]{1,0:T(8,128)(2,1)} %x_hbm.3, bf16[10,512,4096]{2,1,0:T(8,128)(2,1)} %get-tuple-element.15.refs_0_, f8e4m3fn[18,512,4096]{2,1,0:T(32,128)(4,1)} %get-tuple-element.16.refs_1_), custom_call_target="tpu_custom_call", output_to_operand_aliasing={{0}: (1, {}), {1}: (2, {})} | custom-call | bytes 20971520 | tf_op jit(solution)/shard_map/prep/pallas_call | solution.py:100
  42.2 1.1 collective-permute-start.11
  43.4 3.1 %collective-permute-start.22 = (bf16[1024,384]{1,0:T(8,128)(2,1)S(1)}, bf16[1024,384]{1,0:T(8,128)(2,1)S(1)}, u32[]{:S(2)}, u32[]{:S(2)}) collective-permute-start(bf16[1024,384]{1,0:T(8,128)(2,1)S(1)} %pad_maximum_fusion.1.refs_0_), channel_id=1, source_target_pairs={{0,192},{8,72},{16,208},{24,88},{32,224},{40,104},{48,240},{56,120... | collective-permute-start | bytes 2359304 | tf_op jit(solution)/shard_map/ppermute | solution.py:205
  46.5 7.0 %mm.3 = (f32[2,2,128,256]{3,2,1,0:T(8,128)S(1)}, f32[2,2,128,256]{3,2,1,0:T(8,128)S(1)}) custom-call(bf16[10,512,4096]{2,1,0:T(8,128)(2,1)} %get-tuple-element.17.hi_hbm, f8e4m3fn[18,512,4096]{2,1,0:T(32,128)(4,1)} %get-tuple-element.18.lo_hbm, bf16[1024,256]{1,0:T(8,128)(2,1)S(1)} %pad_maximum_fusion.2.refs_0_, ...), custom_call_target="tpu_custom_call" | custom-call | flops 6442450944 | bytes 12582912 | tf_op jit(solution)/shard_map/mm/pallas_call | solution.py:183
  53.6 1.6 %collective-permute-start.6 = (f16[2,2,128,256]{3,2,1,0:T(8,128)(2,1)S(1)}, f16[2,2,128,256]{3,2,1,0:T(8,128)(2,1)S(1)}, u32[]{:S(2)}, u32[]{:S(2)}) collective-permute-start(f16[2,2,128,256]{3,2,1,0:T(8,128)(2,1)S(1)} %convert_element_type.66), channel_id=1, source_target_pairs={{0,1},{1,0},{2,3},{3,2},{4,5},{5,4},{6,7},{7,6},{8,11},{9,10},{10,... | collective-permute-start | bytes 786440 | tf_op jit(solution)/shard_map/ppermute | solution.py:215
  55.2 3.5 %collective-permute-start.21 = (bf16[1024,384]{1,0:T(8,128)(2,1)S(1)}, bf16[1024,384]{1,0:T(8,128)(2,1)}, u32[]{:S(2)}, u32[]{:S(2)}) collective-permute-start(bf16[1024,384]{1,0:T(8,128)(2,1)S(1)} %pad_maximum_fusion.1.refs_0_), channel_id=1, source_target_pairs={{0,8},{8,0},{16,24},{24,16},{32,40},{40,32},{48,56},{56,48},{64,72... | collective-permute-start | bytes 2359304 | tf_op jit(solution)/shard_map/ppermute | solution.py:208
  58.8 0.1 collective-permute-start.13
  58.9 1.8 %collective-permute-done.22.refs_2_ = bf16[1024,384]{1,0:T(8,128)(2,1)S(1)} collective-permute-done((bf16[1024,384]{1,0:T(8,128)(2,1)S(1)}, bf16[1024,384]{1,0:T(8,128)(2,1)S(1)}, u32[]{:S(2)}, u32[]{:S(2)}) %collective-permute-start.22) | collective-permute-done | bytes 786464 | tf_op jit(solution)/shard_map/ppermute | solution.py:205
  60.7 0.8 copy-done.2
  61.5 2.8 %collective-permute-start.7 = (f16[2,128,256]{2,1,0:T(8,128)(2,1)S(1)}, f16[2,128,256]{2,1,0:T(8,128)(2,1)S(1)}, u32[]{:S(2)}, u32[]{:S(2)}) collective-permute-start(f16[2,128,256]{2,1,0:T(8,128)(2,1)S(1)} %fusion.8), channel_id=1, source_target_pairs={{0,3},{1,2},{2,1},{3,0},{4,7},{5,6},{6,5},{7,4},{8,9},{9,8},{10,11... | collective-permute-start | bytes 393224 | tf_op jit(solution)/shard_map/ppermute | solution.py:215
  64.3 3.4 %collective-permute-done.7 = f16[2,128,256]{2,1,0:T(8,128)(2,1)S(1)} collective-permute-done((f16[2,128,256]{2,1,0:T(8,128)(2,1)S(1)}, f16[2,128,256]{2,1,0:T(8,128)(2,1)S(1)}, u32[]{:S(2)}, u32[]{:S(2)}) %collective-permute-start.7) | collective-permute-done | bytes 131104 | tf_op jit(solution)/shard_map/ppermute | solution.py:215
  67.8 1.0 fusion.5
  68.8 5.9 %collective-permute-start.8 = (f16[128,256]{1,0:T(8,128)(2,1)S(1)}, f16[128,256]{1,0:T(8,128)(2,1)S(1)}, u32[]{:S(2)}, u32[]{:S(2)}) collective-permute-start(f16[128,256]{1,0:T(8,128)(2,1)S(1)} %fusion.11), channel_id=1, source_target_pairs={{0,4},{1,5},{2,6},{3,7},{4,0},{5,1},{6,2},{7,3},{8,12},{9,13},{10,... | collective-permute-start | bytes 196616 | tf_op jit(solution)/shard_map/ppermute | solution.py:215
  74.7 0.6 base.1
  75.2 0.1 collective-permute-start.12
  75.4 0.5 collective-permute-start.14
  75.8 1.3 %collective-permute-done.8 = f16[128,256]{1,0:T(8,128)(2,1)S(1)} collective-permute-done((f16[128,256]{1,0:T(8,128)(2,1)S(1)}, f16[128,256]{1,0:T(8,128)(2,1)S(1)}, u32[]{:S(2)}, u32[]{:S(2)}) %collective-permute-start.8) | collective-permute-done | bytes 65568 | tf_op jit(solution)/shard_map/ppermute | solution.py:215
  77.2 10.5 %mm.5 = (f32[2,2,128,384]{3,2,1,0:T(8,128)S(1)}, f32[2,2,128,384]{3,2,1,0:T(8,128)S(1)}) custom-call(bf16[10,512,4096]{2,1,0:T(8,128)(2,1)} %get-tuple-element.17.hi_hbm, f8e4m3fn[18,512,4096]{2,1,0:T(32,128)(4,1)} %get-tuple-element.18.lo_hbm, bf16[1024,384]{1,0:T(8,128)(2,1)S(1)} %pad_maximum_fusion.1.refs_0_, ...), custom_call_target="tpu_custom_call" | custom-call | flops 9663676416 | bytes 12582912 | tf_op jit(solution)/shard_map/mm/pallas_call | solution.py:183
  87.8 0.3 collective-permute-start.24
  88.1 8.6 %mm.4 = (f32[2,2,128,384]{3,2,1,0:T(8,128)S(1)}, f32[2,2,128,384]{3,2,1,0:T(8,128)S(1)}) custom-call(bf16[10,512,4096]{2,1,0:T(8,128)(2,1)} %get-tuple-element.17.hi_hbm, f8e4m3fn[18,512,4096]{2,1,0:T(32,128)(4,1)} %get-tuple-element.18.lo_hbm, bf16[1024,384]{1,0:T(8,128)(2,1)S(1)} %pad_maximum_fusion.refs_0_, ...), custom_call_target="tpu_custom_call" | custom-call | flops 9663676416 | bytes 12582912 | tf_op jit(solution)/shard_map/mm/pallas_call | solution.py:183
  96.8 1.9 %collective-permute-start.15 = (f16[2,2,128,384]{3,2,1,0:T(8,128)(2,1)S(1)}, f16[2,2,128,384]{3,2,1,0:T(8,128)(2,1)S(1)}, u32[]{:S(2)}, u32[]{:S(2)}) collective-permute-start(f16[2,2,128,384]{3,2,1,0:T(8,128)(2,1)S(1)} %convert_element_type.73), channel_id=1, source_target_pairs={{0,1},{1,0},{2,3},{3,2},{4,5},{5,4},{6,7},{7,6},{8,11},{9,10},{10,... | collective-permute-start | bytes 1179656 | tf_op jit(solution)/shard_map/ppermute | solution.py:215
  98.7 0.1 convert_add_fusion
  98.8 2.8 %collective-permute-start.25 = (f16[2,128,384]{2,1,0:T(8,128)(2,1)S(1)}, f16[2,128,384]{2,1,0:T(8,128)(2,1)S(1)}, u32[]{:S(2)}, u32[]{:S(2)}) collective-permute-start(f16[2,128,384]{2,1,0:T(8,128)(2,1)S(1)} %fusion.7), channel_id=1, source_target_pairs={{0,3},{1,2},{2,1},{3,0},{4,7},{5,6},{6,5},{7,4},{8,9},{9,8},{10,11... | collective-permute-start | bytes 589832 | tf_op jit(solution)/shard_map/ppermute | solution.py:215
  101.6 5.1 %collective-permute-done.15 = f16[2,2,128,384]{3,2,1,0:T(8,128)(2,1)S(1)} collective-permute-done((f16[2,2,128,384]{3,2,1,0:T(8,128)(2,1)S(1)}, f16[2,2,128,384]{3,2,1,0:T(8,128)(2,1)S(1)}, u32[]{:S(2)}, u32[]{:S(2)}) %collective-permute-start.15) | collective-permute-done | bytes 393248 | tf_op jit(solution)/shard_map/ppermute | solution.py:215
  106.9 2.7 %collective-permute-start.16 = (f16[2,128,384]{2,1,0:T(8,128)(2,1)S(1)}, f16[2,128,384]{2,1,0:T(8,128)(2,1)S(1)}, u32[]{:S(2)}, u32[]{:S(2)}) collective-permute-start(f16[2,128,384]{2,1,0:T(8,128)(2,1)S(1)} %fusion.6), channel_id=1, source_target_pairs={{0,3},{1,2},{2,1},{3,0},{4,7},{5,6},{6,5},{7,4},{8,9},{9,8},{10,11... | collective-permute-start | bytes 589832 | tf_op jit(solution)/shard_map/ppermute | solution.py:215
  109.6 6.2 %collective-permute-start.26 = (f16[128,384]{1,0:T(8,128)(2,1)S(1)}, f16[128,384]{1,0:T(8,128)(2,1)S(1)}, u32[]{:S(2)}, u32[]{:S(2)}) collective-permute-start(f16[128,384]{1,0:T(8,128)(2,1)S(1)} %fusion.10), channel_id=1, source_target_pairs={{0,4},{1,5},{2,6},{3,7},{4,0},{5,1},{6,2},{7,3},{8,12},{9,13},{10,... | collective-permute-start | bytes 294920 | tf_op jit(solution)/shard_map/ppermute | solution.py:215
  115.9 3.6 %collective-permute-start.17 = (f16[128,384]{1,0:T(8,128)(2,1)S(1)}, f16[128,384]{1,0:T(8,128)(2,1)S(1)}, u32[]{:S(2)}, u32[]{:S(2)}) collective-permute-start(f16[128,384]{1,0:T(8,128)(2,1)S(1)} %fusion.9), channel_id=1, source_target_pairs={{0,4},{1,5},{2,6},{3,7},{4,0},{5,1},{6,2},{7,3},{8,12},{9,13},{10,... | collective-permute-start | bytes 294920 | tf_op jit(solution)/shard_map/ppermute | solution.py:215
  119.5 0.2 collective-permute-done.26
  119.7 5.4 %collective-permute-done.17 = f16[128,384]{1,0:T(8,128)(2,1)S(1)} collective-permute-done((f16[128,384]{1,0:T(8,128)(2,1)S(1)}, f16[128,384]{1,0:T(8,128)(2,1)S(1)}, u32[]{:S(2)}, u32[]{:S(2)}) %collective-permute-start.17) | collective-permute-done | bytes 98336 | tf_op jit(solution)/shard_map/ppermute | solution.py:215
  125.2 1.0 fusion.2
  (52 shorter events, 1.0 us)
Async XLA Ops:
  0.8 5.5 %collective-permute-start = (bf16[128,256]{1,0:T(8,128)(2,1)S(1)}, bf16[128,256]{1,0:T(8,128)(2,1)S(1)}, u32[]{:S(2)}, u32[]{:S(2)}) collective-permute-start(bf16[128,256]{1,0:T(8,128)(2,1)S(1)} %slice.30), channel_id=1, source_target_pairs={{0,32},{8,24},{16,48},{24,8},{32,0},{40,56},{48,16},{56,40},{64,96... | collective-permute-start | bytes 196616 | tf_op jit(solution)/shard_map/ppermute | solution.py:205
  6.4 5.2 %collective-permute-start.1 = (bf16[256,256]{1,0:T(8,128)(2,1)S(1)}, bf16[256,256]{1,0:T(8,128)(2,1)S(1)}, u32[]{:S(2)}, u32[]{:S(2)}) collective-permute-start(bf16[256,256]{1,0:T(8,128)(2,1)S(1)} %pad_maximum_fusion.8), channel_id=1, source_target_pairs={{0,16},{8,40},{16,0},{24,56},{32,48},{40,8},{48,32},{56,24},{64,80... | collective-permute-start | bytes 393224 | tf_op jit(solution)/shard_map/ppermute | solution.py:205
  11.6 7.0 %collective-permute-start.2 = (bf16[512,256]{1,0:T(8,128)(2,1)S(1)}, bf16[512,256]{1,0:T(8,128)(2,1)S(1)}, u32[]{:S(2)}, u32[]{:S(2)}) collective-permute-start(bf16[512,256]{1,0:T(8,128)(2,1)S(1)} %pad_maximum_fusion.5), channel_id=1, source_target_pairs={{0,64},{8,200},{16,80},{24,216},{32,96},{40,232},{48,112},{56,248}... | collective-permute-start | bytes 786440 | tf_op jit(solution)/shard_map/ppermute | solution.py:205
  15.2 6.1 %collective-permute-start.18 = (bf16[128,384]{1,0:T(8,128)(2,1)S(1)}, bf16[128,384]{1,0:T(8,128)(2,1)S(1)}, u32[]{:S(2)}, u32[]{:S(2)}) collective-permute-start(bf16[128,384]{1,0:T(8,128)(2,1)S(1)} %get-tuple-element.26), channel_id=1, source_target_pairs={{0,32},{8,24},{16,48},{24,8},{32,0},{40,56},{48,16},{56,40},{64,96... | collective-permute-start | bytes 294920 | tf_op jit(solution)/shard_map/ppermute | solution.py:205
  18.6 11.4 %collective-permute-start.4 = (bf16[1024,256]{1,0:T(8,128)(2,1)S(1)}, bf16[1024,256]{1,0:T(8,128)(2,1)S(1)}, u32[]{:S(2)}, u32[]{:S(2)}) collective-permute-start(bf16[1024,256]{1,0:T(8,128)(2,1)S(1)} %pad_maximum_fusion.2.refs_0_), channel_id=1, source_target_pairs={{0,192},{8,72},{16,208},{24,88},{32,224},{40,104},{48,240},{56,120... | collective-permute-start | bytes 1572872 | tf_op jit(solution)/shard_map/ppermute | solution.py:205
  21.3 7.5 %collective-permute-start.19 = (bf16[256,384]{1,0:T(8,128)(2,1)S(1)}, bf16[256,384]{1,0:T(8,128)(2,1)S(1)}, u32[]{:S(2)}, u32[]{:S(2)}) collective-permute-start(bf16[256,384]{1,0:T(8,128)(2,1)S(1)} %pad_maximum_fusion.7), channel_id=1, source_target_pairs={{0,16},{8,40},{16,0},{24,56},{32,48},{40,8},{48,32},{56,24},{64,80... | collective-permute-start | bytes 589832 | tf_op jit(solution)/shard_map/ppermute | solution.py:205
  21.6 8.9 %collective-permute-start.9 = (bf16[128,384]{1,0:T(8,128)(2,1)S(1)}, bf16[128,384]{1,0:T(8,128)(2,1)S(1)}, u32[]{:S(2)}, u32[]{:S(2)}) collective-permute-start(bf16[128,384]{1,0:T(8,128)(2,1)S(1)} %get-tuple-element.25), channel_id=1, source_target_pairs={{0,32},{8,24},{16,48},{24,8},{32,0},{40,56},{48,16},{56,40},{64,96... | collective-permute-start | bytes 294920 | tf_op jit(solution)/shard_map/ppermute | solution.py:205
  28.9 14.4 %collective-permute-start.20 = (bf16[512,384]{1,0:T(8,128)(2,1)S(1)}, bf16[512,384]{1,0:T(8,128)(2,1)S(1)}, u32[]{:S(2)}, u32[]{:S(2)}) collective-permute-start(bf16[512,384]{1,0:T(8,128)(2,1)S(1)} %pad_maximum_fusion.4), channel_id=1, source_target_pairs={{0,64},{8,200},{16,80},{24,216},{32,96},{40,232},{48,112},{56,248}... | collective-permute-start | bytes 1179656 | tf_op jit(solution)/shard_map/ppermute | solution.py:205
  30.1 16.4 %collective-permute-start.3 = (bf16[1024,256]{1,0:T(8,128)(2,1)S(1)}, bf16[1024,256]{1,0:T(8,128)(2,1)S(1)}, u32[]{:S(2)}, u32[]{:S(2)}) collective-permute-start(bf16[1024,256]{1,0:T(8,128)(2,1)S(1)} %pad_maximum_fusion.2.refs_0_), channel_id=1, source_target_pairs={{0,8},{8,0},{16,24},{24,16},{32,40},{40,32},{48,56},{56,48},{64,72... | collective-permute-start | bytes 1572872 | tf_op jit(solution)/shard_map/ppermute | solution.py:208
  30.1 16.4 %collective-permute-start.5 = (bf16[1024,256]{1,0:T(8,128)(2,1)S(1)}, bf16[1024,256]{1,0:T(8,128)(2,1)S(1)}, u32[]{:S(2)}, u32[]{:S(2)}) collective-permute-start(bf16[1024,256]{1,0:T(8,128)(2,1)S(1)} %collective-permute-done.4.refs_2_), channel_id=1, source_target_pairs={{0,8},{8,0},{16,24},{24,16},{32,40},{40,32},{48,56},{56,48},{64,72... | collective-permute-start | bytes 1572872 | tf_op jit(solution)/shard_map/ppermute | solution.py:209
  30.6 11.6 %collective-permute-start.10 = (bf16[256,384]{1,0:T(8,128)(2,1)S(1)}, bf16[256,384]{1,0:T(8,128)(2,1)S(1)}, u32[]{:S(2)}, u32[]{:S(2)}) collective-permute-start(bf16[256,384]{1,0:T(8,128)(2,1)S(1)} %pad_maximum_fusion.6), channel_id=1, source_target_pairs={{0,16},{8,40},{16,0},{24,56},{32,48},{40,8},{48,32},{56,24},{64,80... | collective-permute-start | bytes 589832 | tf_op jit(solution)/shard_map/ppermute | solution.py:205
  42.2 16.4 %collective-permute-start.11 = (bf16[512,384]{1,0:T(8,128)(2,1)S(1)}, bf16[512,384]{1,0:T(8,128)(2,1)S(1)}, u32[]{:S(2)}, u32[]{:S(2)}) collective-permute-start(bf16[512,384]{1,0:T(8,128)(2,1)S(1)} %pad_maximum_fusion.3), channel_id=1, source_target_pairs={{0,64},{8,200},{16,80},{24,216},{32,96},{40,232},{48,112},{56,248}... | collective-permute-start | bytes 1179656 | tf_op jit(solution)/shard_map/ppermute | solution.py:205
  43.4 17.2 %collective-permute-start.22 = (bf16[1024,384]{1,0:T(8,128)(2,1)S(1)}, bf16[1024,384]{1,0:T(8,128)(2,1)S(1)}, u32[]{:S(2)}, u32[]{:S(2)}) collective-permute-start(bf16[1024,384]{1,0:T(8,128)(2,1)S(1)} %pad_maximum_fusion.1.refs_0_), channel_id=1, source_target_pairs={{0,192},{8,72},{16,208},{24,88},{32,224},{40,104},{48,240},{56,120... | collective-permute-start | bytes 2359304 | tf_op jit(solution)/shard_map/ppermute | solution.py:205
  53.6 7.0 %collective-permute-start.6 = (f16[2,2,128,256]{3,2,1,0:T(8,128)(2,1)S(1)}, f16[2,2,128,256]{3,2,1,0:T(8,128)(2,1)S(1)}, u32[]{:S(2)}, u32[]{:S(2)}) collective-permute-start(f16[2,2,128,256]{3,2,1,0:T(8,128)(2,1)S(1)} %convert_element_type.66), channel_id=1, source_target_pairs={{0,1},{1,0},{2,3},{3,2},{4,5},{5,4},{6,7},{7,6},{8,11},{9,10},{10,... | collective-permute-start | bytes 786440 | tf_op jit(solution)/shard_map/ppermute | solution.py:215
  55.2 22.0 %collective-permute-start.21 = (bf16[1024,384]{1,0:T(8,128)(2,1)S(1)}, bf16[1024,384]{1,0:T(8,128)(2,1)}, u32[]{:S(2)}, u32[]{:S(2)}) collective-permute-start(bf16[1024,384]{1,0:T(8,128)(2,1)S(1)} %pad_maximum_fusion.1.refs_0_), channel_id=1, source_target_pairs={{0,8},{8,0},{16,24},{24,16},{32,40},{40,32},{48,56},{56,48},{64,72... | collective-permute-start | bytes 2359304 | tf_op jit(solution)/shard_map/ppermute | solution.py:208
  58.7 15.9 %copy-start = (f32[512]{0:T(512)S(1)}, f32[512]{0:T(512)}, u32[]{:S(2)}) copy-start(f32[512]{0:T(512)} %param.10) | copy-start | bytes 6148
  58.7 15.9 %copy-start.1 = (f32[64]{0:T(128)S(1)}, f32[64]{0:T(128)}, u32[]{:S(2)}) copy-start(f32[64]{0:T(128)} %occ.1) | copy-start | bytes 772
  58.8 16.6 %collective-permute-start.13 = (bf16[1024,384]{1,0:T(8,128)(2,1)S(1)}, bf16[1024,384]{1,0:T(8,128)(2,1)S(1)}, u32[]{:S(2)}, u32[]{:S(2)}) collective-permute-start(bf16[1024,384]{1,0:T(8,128)(2,1)S(1)} %pad_maximum_fusion.refs_0_), channel_id=1, source_target_pairs={{0,192},{8,72},{16,208},{24,88},{32,224},{40,104},{48,240},{56,120... | collective-permute-start | bytes 2359304 | tf_op jit(solution)/shard_map/ppermute | solution.py:205
  60.6 16.6 %collective-permute-start.23 = (bf16[1024,384]{1,0:T(8,128)(2,1)S(1)}, bf16[1024,384]{1,0:T(8,128)(2,1)}, u32[]{:S(2)}, u32[]{:S(2)}) collective-permute-start(bf16[1024,384]{1,0:T(8,128)(2,1)S(1)} %collective-permute-done.22.refs_2_), channel_id=1, source_target_pairs={{0,8},{8,0},{16,24},{24,16},{32,40},{40,32},{48,56},{56,48},{64,72... | collective-permute-start | bytes 2359304 | tf_op jit(solution)/shard_map/ppermute | solution.py:209
  60.7 0.8 copy-start.2
  61.5 6.3 %collective-permute-start.7 = (f16[2,128,256]{2,1,0:T(8,128)(2,1)S(1)}, f16[2,128,256]{2,1,0:T(8,128)(2,1)S(1)}, u32[]{:S(2)}, u32[]{:S(2)}) collective-permute-start(f16[2,128,256]{2,1,0:T(8,128)(2,1)S(1)} %fusion.8), channel_id=1, source_target_pairs={{0,3},{1,2},{2,1},{3,0},{4,7},{5,6},{6,5},{7,4},{8,9},{9,8},{10,11... | collective-permute-start | bytes 393224 | tf_op jit(solution)/shard_map/ppermute | solution.py:215
  68.8 8.4 %collective-permute-start.8 = (f16[128,256]{1,0:T(8,128)(2,1)S(1)}, f16[128,256]{1,0:T(8,128)(2,1)S(1)}, u32[]{:S(2)}, u32[]{:S(2)}) collective-permute-start(f16[128,256]{1,0:T(8,128)(2,1)S(1)} %fusion.11), channel_id=1, source_target_pairs={{0,4},{1,5},{2,6},{3,7},{4,0},{5,1},{6,2},{7,3},{8,12},{9,13},{10,... | collective-permute-start | bytes 196616 | tf_op jit(solution)/shard_map/ppermute | solution.py:215
  75.2 12.9 %collective-permute-start.12 = (bf16[1024,384]{1,0:T(8,128)(2,1)S(1)}, bf16[1024,384]{1,0:T(8,128)(2,1)S(1)}, u32[]{:S(2)}, u32[]{:S(2)}) collective-permute-start(bf16[1024,384]{1,0:T(8,128)(2,1)S(1)} %pad_maximum_fusion.refs_0_), channel_id=1, source_target_pairs={{0,8},{8,0},{16,24},{24,16},{32,40},{40,32},{48,56},{56,48},{64,72... | collective-permute-start | bytes 2359304 | tf_op jit(solution)/shard_map/ppermute | solution.py:208
  75.4 12.8 %collective-permute-start.14 = (bf16[1024,384]{1,0:T(8,128)(2,1)S(1)}, bf16[1024,384]{1,0:T(8,128)(2,1)S(1)}, u32[]{:S(2)}, u32[]{:S(2)}) collective-permute-start(bf16[1024,384]{1,0:T(8,128)(2,1)S(1)} %collective-permute-done.13.refs_2_), channel_id=1, source_target_pairs={{0,8},{8,0},{16,24},{24,16},{32,40},{40,32},{48,56},{56,48},{64,72... | collective-permute-start | bytes 2359304 | tf_op jit(solution)/shard_map/ppermute | solution.py:209
  87.8 10.9 %collective-permute-start.24 = (f16[2,2,128,384]{3,2,1,0:T(8,128)(2,1)S(1)}, f16[2,2,128,384]{3,2,1,0:T(8,128)(2,1)S(1)}, u32[]{:S(2)}, u32[]{:S(2)}) collective-permute-start(f16[2,2,128,384]{3,2,1,0:T(8,128)(2,1)S(1)} %convert_element_type.80), channel_id=1, source_target_pairs={{0,1},{1,0},{2,3},{3,2},{4,5},{5,4},{6,7},{7,6},{8,11},{9,10},{10,... | collective-permute-start | bytes 1179656 | tf_op jit(solution)/shard_map/ppermute | solution.py:215
  96.8 10.0 %collective-permute-start.15 = (f16[2,2,128,384]{3,2,1,0:T(8,128)(2,1)S(1)}, f16[2,2,128,384]{3,2,1,0:T(8,128)(2,1)S(1)}, u32[]{:S(2)}, u32[]{:S(2)}) collective-permute-start(f16[2,2,128,384]{3,2,1,0:T(8,128)(2,1)S(1)} %convert_element_type.73), channel_id=1, source_target_pairs={{0,1},{1,0},{2,3},{3,2},{4,5},{5,4},{6,7},{7,6},{8,11},{9,10},{10,... | collective-permute-start | bytes 1179656 | tf_op jit(solution)/shard_map/ppermute | solution.py:215
  98.8 10.8 %collective-permute-start.25 = (f16[2,128,384]{2,1,0:T(8,128)(2,1)S(1)}, f16[2,128,384]{2,1,0:T(8,128)(2,1)S(1)}, u32[]{:S(2)}, u32[]{:S(2)}) collective-permute-start(f16[2,128,384]{2,1,0:T(8,128)(2,1)S(1)} %fusion.7), channel_id=1, source_target_pairs={{0,3},{1,2},{2,1},{3,0},{4,7},{5,6},{6,5},{7,4},{8,9},{9,8},{10,11... | collective-permute-start | bytes 589832 | tf_op jit(solution)/shard_map/ppermute | solution.py:215
  106.9 18.3 %copy-start.3 = (f32[128,1024]{1,0:T(8,128)S(1)}, f32[128,1024]{1,0:T(8,128)}, u32[]{:S(2)}) copy-start(f32[128,1024]{1,0:T(8,128)} %param.8) | copy-start | bytes 1572868
  106.9 18.3 %copy-start.4 = (f32[1024]{0:T(1024)S(1)}, f32[1024]{0:T(1024)}, u32[]{:S(2)}) copy-start(f32[1024]{0:T(1024)} %param.11) | copy-start | bytes 12292
  106.9 8.9 %collective-permute-start.16 = (f16[2,128,384]{2,1,0:T(8,128)(2,1)S(1)}, f16[2,128,384]{2,1,0:T(8,128)(2,1)S(1)}, u32[]{:S(2)}, u32[]{:S(2)}) collective-permute-start(f16[2,128,384]{2,1,0:T(8,128)(2,1)S(1)} %fusion.6), channel_id=1, source_target_pairs={{0,3},{1,2},{2,1},{3,0},{4,7},{5,6},{6,5},{7,4},{8,9},{9,8},{10,11... | collective-permute-start | bytes 589832 | tf_op jit(solution)/shard_map/ppermute | solution.py:215
  109.6 10.0 %collective-permute-start.26 = (f16[128,384]{1,0:T(8,128)(2,1)S(1)}, f16[128,384]{1,0:T(8,128)(2,1)S(1)}, u32[]{:S(2)}, u32[]{:S(2)}) collective-permute-start(f16[128,384]{1,0:T(8,128)(2,1)S(1)} %fusion.10), channel_id=1, source_target_pairs={{0,4},{1,5},{2,6},{3,7},{4,0},{5,1},{6,2},{7,3},{8,12},{9,13},{10,... | collective-permute-start | bytes 294920 | tf_op jit(solution)/shard_map/ppermute | solution.py:215
  115.9 9.2 %collective-permute-start.17 = (f16[128,384]{1,0:T(8,128)(2,1)S(1)}, f16[128,384]{1,0:T(8,128)(2,1)S(1)}, u32[]{:S(2)}, u32[]{:S(2)}) collective-permute-start(f16[128,384]{1,0:T(8,128)(2,1)S(1)} %fusion.9), channel_id=1, source_target_pairs={{0,4},{1,5},{2,6},{3,7},{4,0},{5,1},{6,2},{7,3},{8,12},{9,13},{10,... | collective-permute-start | bytes 294920 | tf_op jit(solution)/shard_map/ppermute | solution.py:215
